TPU v7x, 32 devices: a whole 2x2x4 slice. The times are simulated.
32 devices in a mesh: dp: 4 (over z), owner: 2 (over x), tensor: 4 (over y, core).
Axes of the slice: x: 2, y: 2, z: 4, core: 2. Of those that a mesh axis runs over, the one named last changes fastest.
Arguments:
- train_act: bfloat16 [8, 512, 8192], P(('dp', 'owner'), None, 'tensor'), may hold values from -6 to 6
- train_grad: bfloat16 [8, 512, 28672], P(('dp', 'owner'), None, 'tensor'), may hold values from -0.0234375 to 0.0234375
- query_act: bfloat16 [8, 128, 8192], P(('dp', 'owner'), None, 'tensor'), may hold values from -6 to 6
- query_grad: bfloat16 [8, 128, 28672], P(('dp', 'owner'), None, 'tensor'), may hold values from -0.0234375 to 0.0234375
- basis_out: bfloat16 [28672, 512], P('tensor', 'owner'), may hold values from -0.03125 to 0.03125
- basis_in: bfloat16 [8192, 512], P('tensor', 'owner'), may hold values from -0.0625 to 0.0625
- eigen_corr: float32 [512, 512], P('tensor'), may hold values from 0.05 to 5
- seq_lengths: int32 [8], P(('dp', 'owner')), may hold values from 1 to 512, as said below
- seq_buckets: int32 [8], P(('dp', 'owner')), may hold values from 0 to 3, as said below
Outputs:
- influence: float32 [8, 8], P(('dp', 'owner'))
Inputs may be any that keep to these rules, and one draw needn't show every extreme that they name: `seq_lengths`: some sequence has exactly 512 real tokens. (seq_buckets[n] + 1) * 128 >= seq_lengths[n]; bucket 0 and bucket 3 (the last) both occur.
All inputs are finite; a program needn't handle non-finite values.
Results may differ from a plain program's by a relative error of at most 0.008.
Values may be sent and summed in bfloat16 or wider, within the bound.
No kernel may reach another device: no remote copies, remote signals or barrier semaphores. Data moves between devices by JAX's collectives and lax.ppermute only.
A program may use at most 128 MiB of HBM per device.

v0:
```python
import jax
import jax.numpy as jnp
from jax import lax
from jax.experimental import pallas as pl
from jax.experimental.pallas import tpu as pltpu
from jax.sharding import PartitionSpec as P


LEN = 512
NBUCK = 4
damping = 0.05
PARITY, PLACE, OWNER, BEGIN, END, HERE = range(6)


def block_of(depth):
    return next(b for b in (1792, 1024, 512, 256, depth) if depth % b == 0)


def flip(array, axis, mask):
    size = lax.axis_size(axis)
    return lax.ppermute(array, axis, [(i, i ^ mask) for i in range(size)])


def cut(where, basis, size, spans):
    block = min(block_of(size), 512)
    width = basis.shape[1]

    def body(where_ref, *refs):
        for source, target in zip(refs[: len(spans)], refs[len(spans) :]):
            target[...] = source[...]

    def span(first, added):
        return lambda k, where_ref: (first // block + where_ref[PARITY] * (added // block) + k, 0)

    return pl.pallas_call(
        body,
        out_shape=[jax.ShapeDtypeStruct((size, width), basis.dtype) for _ in spans],
        grid_spec=pltpu.PrefetchScalarGridSpec(
            num_scalar_prefetch=1,
            grid=(size // block,),
            in_specs=[pl.BlockSpec((block, width), span(*s)) for s in spans],
            out_specs=[pl.BlockSpec((block, width), lambda k, where_ref: (k, 0)) for _ in spans],
        ),
    )(where, *[basis] * len(spans))


def rotate_own(act, qact, basis_in, grad, qgrad, basis_out):
    total, qtotal, half = grad.shape[0], qgrad.shape[0], basis_in.shape[1]
    deep = block_of(basis_out.shape[0])
    steps = basis_out.shape[0] // deep
    shallow = basis_in.shape[0] // steps

    def body(a, qa, bi, g, qg, bo, out_ref):
        @pl.when(pl.program_id(0) == 0)
        def _():
            out_ref[...] = jnp.zeros_like(out_ref)

        for rows, qrows, piece, cols in ((a, qa, bi, slice(0, half)), (g, qg, bo, slice(half, 2 * half))):
            held = piece[...]
            out_ref[:total, cols] += jnp.dot(rows[...], held, preferred_element_type=jnp.float32)
            out_ref[total:, cols] += jnp.dot(qrows[...], held, preferred_element_type=jnp.float32)

    def specs(block):
        return [
            pl.BlockSpec((total, block), lambda k: (0, k)),
            pl.BlockSpec((qtotal, block), lambda k: (0, k)),
            pl.BlockSpec((block, half), lambda k: (k, 0)),
        ]

    depth = basis_in.shape[0] + basis_out.shape[0]
    return pl.pallas_call(
        body,
        out_shape=jax.ShapeDtypeStruct((total + qtotal, 2 * half), jnp.float32),
        grid=(steps,),
        in_specs=specs(shallow) + specs(deep),
        out_specs=pl.BlockSpec((total + qtotal, 2 * half), lambda k: (0, 0)),
        cost_estimate=pl.CostEstimate(
            flops=2 * (total + qtotal) * half * depth, bytes_accessed=2 * depth * (total + qtotal + half), transcendentals=0
        ),
    )(act, qact, basis_in, grad, qgrad, basis_out)


def rotate(where, rows, qrows, parts, acc=None, ways=None):
    pieces = [piece for piece, _, _ in parts]
    count, cols, depth = len(pieces), pieces[0].shape[1], pieces[0].shape[0]
    block = min(block_of(depth), 512)
    steps = depth // block
    total, qtotal = rows.shape[0], qrows.shape[0]
    height = total + qtotal

    def body(where_ref, *refs):
        rows_refs, qrows_refs = refs[:count], refs[count : 2 * count]
        piece_refs = refs[2 * count : 3 * count]
        out_ref = refs[-1] if ways else refs[3 * count + (acc is not None)]

        @pl.when(pl.program_id(0) == 0)
        def _():
            out_ref[...] = jnp.zeros_like(out_ref) if acc is None else refs[3 * count][...]

        for n in range(count):
            piece = piece_refs[n][...]
            out_ref[:total, :] += jnp.dot(rows_refs[n][...], piece, preferred_element_type=jnp.float32)
            out_ref[total:, :] += jnp.dot(qrows_refs[n][...], piece, preferred_element_type=jnp.float32)

        if ways:

            @pl.when(pl.program_id(0) == steps - 1)
            def _():
                outs = refs[3 * count + (acc is not None) : -1]
                outs[0][...] = out_ref[:total, :]
                share = qtotal // ways
                for k in range(ways):
                    begin = pl.multiple_of(total + (where_ref[PLACE] ^ k) * share, share)
                    outs[1 + k][...] = out_ref[pl.ds(begin, share), :]

    def span(n):
        _, first, added = parts[n]
        return lambda k, where_ref: (0, first // block + where_ref[PARITY] * (added // block) + k)

    def whole(shape):
        return pl.BlockSpec(shape, lambda k, where_ref: (0, 0))

    in_specs = [pl.BlockSpec((total, block), span(n)) for n in range(count)]
    in_specs += [pl.BlockSpec((qtotal, block), span(n)) for n in range(count)]
    in_specs += [pl.BlockSpec((block, cols), lambda k, where_ref: (k, 0)) for _ in range(count)]
    operands = [rows] * count + [qrows] * count + pieces
    if acc is not None:
        in_specs.append(whole((height, cols)))
        operands.append(acc)
    shapes, scratch = [(height, cols)], []
    if ways:
        shapes = [(total, cols)] + [(qtotal // ways, cols)] * ways
        scratch = [pltpu.VMEM((height, cols), jnp.float32)]
    outs = pl.pallas_call(
        body,
        out_shape=[jax.ShapeDtypeStruct(shape, jnp.float32) for shape in shapes],
        grid_spec=pltpu.PrefetchScalarGridSpec(
            num_scalar_prefetch=1,
            grid=(steps,),
            in_specs=in_specs,
            out_specs=[whole(shape) for shape in shapes],
            scratch_shapes=scratch,
        ),
        cost_estimate=pl.CostEstimate(
            flops=2 * height * cols * depth * count,
            bytes_accessed=2 * count * depth * (height + cols) + 8 * height * cols,
            transcendentals=0,
        ),
    )(where, *operands)
    return outs if ways else outs[0]


def weigh(where, own, inner, outer, query, corr):
    length, half = outer[0].shape
    places, share, _ = query[0].shape
    rows = places * share
    blocks, tall = len(corr), corr[0].shape[0]

    def body(where_ref, own_a, own_b, in_a, in_b, out_a, out_b, qa, qb, *refs):
        corr_refs, (far_ref, near_ref, part_ref), curv = refs[:blocks], refs[blocks:-1], refs[-1]
        side, begin, end = where_ref[OWNER], where_ref[BEGIN], where_ref[END]
        for k in range(blocks):
            curv[pl.ds(pl.multiple_of((where_ref[PLACE] ^ k) * tall, tall), tall), :] = corr_refs[k][...]

        def rounded(a, b, cols):
            return (a[:length, cols] + b[:length, cols].astype(jnp.float32)).astype(jnp.bfloat16)

        everything, first, second = slice(None), slice(0, half), slice(half, 2 * half)
        ins = (rounded(own_a, own_b, first), rounded(in_a, in_b, everything))
        outs = (rounded(own_a, own_b, second), rounded(out_a, out_b, everything))
        position = lax.broadcasted_iota(jnp.int32, (length, half), 0)
        live = ((position >= begin) & (position < end)).astype(jnp.bfloat16)
        near = qa[...].reshape(rows, 3 * half)
        far = qb[...].reshape(rows, 3 * half)
        qins = (
            jnp.concatenate([near[:, :half], far[:, 2 * half :]], 0),
            jnp.concatenate([near[:, 2 * half :], far[:, :half]], 0),
        )
        moved = []
        for h in range(2):
            masked = outs[h] * live
            total = jnp.zeros((2 * rows, half), jnp.float32)
            for j in range(2):
                rot = lax.dot_general(
                    masked, ins[j], (((0,), (0,)), ((), ())), preferred_element_type=jnp.float32
                )
                rot = rot.astype(jnp.bfloat16).astype(jnp.float32)
                weight = rot / (
                    curv[
                        pl.ds(pl.multiple_of((side ^ h) * half, half), half),
                        pl.ds(pl.multiple_of((side ^ j) * half, half), half),
                    ]
                    + damping
                )
                high = weight.astype(jnp.bfloat16)
                low = (weight - high.astype(jnp.float32)).astype(jnp.bfloat16)
                for part in (high, low):
                    total += lax.dot_general(
                        qins[j], part, (((1,), (1,)), ((), ())), preferred_element_type=jnp.float32
                    )
            moved.append(total)
        near_ref[...] = moved[1][:rows]
        far_ref[...] = moved[0][rows:]
        part_ref[:places, :] = row_sums(moved[0][:rows] * near[:, half : 2 * half].astype(jnp.float32), places)
        part_ref[places:, :] = row_sums(moved[1][rows:] * far[:, half : 2 * half].astype(jnp.float32), places)

    vmem = pl.BlockSpec(memory_space=pltpu.VMEM)
    product = jax.ShapeDtypeStruct((rows, half), jnp.float32)
    return pl.pallas_call(
        body,
        out_shape=[product, product, jax.ShapeDtypeStruct((2 * places, half), jnp.float32)],
        in_specs=[pl.BlockSpec(memory_space=pltpu.SMEM)] + [vmem] * (8 + blocks),
        out_specs=[vmem] * 3,
        scratch_shapes=[pltpu.VMEM((blocks * tall, corr[0].shape[1]), jnp.float32)],
    )(where, *own, *inner, *outer, *query, *corr)


def row_sums(values, places):
    rows, width = values.shape
    return jnp.sum(values.reshape(places, rows // places, width), axis=1)


def gather_scores(where, moved, late, masks):
    far, near, part = moved
    places, share, half = late[0].shape
    count = 2 * places

    def body(where_ref, far_ref, near_ref, part_ref, la, lb, out_ref):
        def met(product, block):
            return row_sums(product[...] * block[...].reshape(places * share, half).astype(jnp.float32), places)

        sums = part_ref[...] + jnp.concatenate([met(near_ref, la), met(far_ref, lb)], 0)
        sums = jnp.sum(sums, axis=1, keepdims=True)
        index = lax.broadcasted_iota(jnp.int32, (count, 128), 0)
        query = jnp.zeros((count, 128), jnp.int32)
        for n, mask in enumerate(masks):
            query = jnp.where(index == n, mask, query)
        query = query ^ where_ref[HERE]
        hits = lax.broadcasted_iota(jnp.int32, (count, 128), 1) == query
        line = jnp.sum(jnp.where(hits, sums, 0.0), axis=0, keepdims=True)
        out_ref[...] = jnp.broadcast_to(line, out_ref.shape)

    vmem = pl.BlockSpec(memory_space=pltpu.VMEM)
    return pl.pallas_call(
        body,
        out_shape=jax.ShapeDtypeStruct((8, 128), jnp.float32),
        in_specs=[pl.BlockSpec(memory_space=pltpu.SMEM)] + [vmem] * 5,
        out_specs=vmem,
    )(where, far, near, part, *late)


def on_device(
    train_act,
    train_grad,
    query_act,
    query_grad,
    basis_out,
    basis_in,
    eigen_corr,
    seq_lengths,
    seq_buckets,
):
    dp, owner, place = lax.axis_index("dp"), lax.axis_index("owner"), lax.axis_index("tensor")
    tensor_size, dp_size = lax.axis_size("tensor"), lax.axis_size("dp")
    grad, act = train_grad[0], train_act[0]
    qgrad, qact = query_grad[0], query_act[0]
    length, qlength = grad.shape[0], qgrad.shape[0]
    share = qlength // tensor_size
    parity = dp % 2
    bf16, f32 = jnp.bfloat16, jnp.float32
    bits = [1 << n for n in range(tensor_size.bit_length() - 1)]

    ends = (seq_buckets[0] + 1) * (LEN // NBUCK)
    here = dp * lax.axis_size("owner") + owner
    where = jnp.stack([parity, place, owner, ends - seq_lengths[0], ends, here]).astype(jnp.int32)

    width_in, width_out = basis_in.shape[0], basis_out.shape[0]
    step = width_out // 7

    def fetch(mine, base, size):
        direct = flip(mine, "owner", 1)
        relayed = flip(direct, "dp", 1)
        return (direct, base, size), (relayed, base + size, -size)

    first = lax.dynamic_slice_in_dim(basis_in, parity * (width_in // 2), width_in // 2, 0)
    in_parts = fetch(first, 0, width_in // 2)
    spans = [(2 * n * step, step) for n in range(3)] + [(6 * step, 0)]
    shares = [*cut(where, basis_out, step, spans[:1])]
    *later, last = cut(where, basis_out, step, spans[1:])
    shares += later
    chunks = [fetch(shares[n], 2 * n * step, step) for n in range(3)]
    last = (flip(last, "owner", 1), 6 * step, 0)

    def shared(value):
        for bit in bits[:-1]:
            value = value + flip(value, "tensor", bit)
        return value, flip(value.astype(bf16), "tensor", bits[-1])

    own = rotate_own(act, qact, basis_in, grad, qgrad, basis_out)
    own = shared(own)
    inner = rotate(where, act, qact, in_parts)
    inner = shared(inner)

    corr = [eigen_corr]
    for k in range(1, tensor_size):
        corr.append(flip(eigen_corr, "tensor", k))

    groups = []
    bit = 1
    while bit < dp_size:
        ways = min(4, dp_size // bit)
        groups.append([("dp", bit * k, bit * k * lax.axis_size("owner")) for k in range(1, ways)])
        bit *= ways
    groups.append([("owner", 1, 1)])

    def everyone(block):
        gathered = block[None]
        for group in groups:
            peers = []
            for axis, mask, _ in group:
                peers.append(flip(gathered, axis, mask))
            if group is groups[-1]:
                return gathered, peers[0]
            gathered = jnp.concatenate([gathered, *peers], 0)

    masks = [0]
    for group in groups:
        masks = [m ^ added for added in [0] + [g for _, _, g in group] for m in masks]

    def my_rows(pair):
        a, b = (lax.dynamic_slice_in_dim(v, length + place * share, share, 0) for v in pair)
        return (a + b.astype(f32)).astype(bf16)

    early = everyone(jnp.concatenate([my_rows(own), my_rows(inner)], 1))

    acc = None
    for parts in (chunks[0], chunks[1], [chunks[2][0], last]):
        acc = rotate(where, grad, qgrad, parts, acc)
    outer, *qouter = rotate(where, grad, qgrad, [chunks[2][1]], acc, ways=tensor_size)
    qsum = qouter[0]
    for k in range(1, tensor_size):
        qsum = qsum + flip(qouter[k], "tensor", k)
    late = everyone(qsum.astype(bf16))
    outer = shared(outer)

    moved = weigh(where, own, inner, outer, early, corr)
    scores = gather_scores(where, moved, late, masks)
    pieces = [scores]
    for k in range(1, tensor_size):
        pieces.append(flip(scores, "tensor", k))
    while len(pieces) > 1:
        pieces = [a + b for a, b in zip(pieces[::2], pieces[1::2])]
    return pieces[0][:1, : 2 * late[0].shape[0]]


def solution(mesh):
    return jax.shard_map(
        on_device,
        mesh=mesh,
        in_specs=(
            P(("dp", "owner"), None, "tensor"),
            P(("dp", "owner"), None, "tensor"),
            P(("dp", "owner"), None, "tensor"),
            P(("dp", "owner"), None, "tensor"),
            P("tensor", "owner"),
            P("tensor", "owner"),
            P("tensor", None),
            P(("dp", "owner")),
            P(("dp", "owner")),
        ),
        out_specs=P(("dp", "owner"), None),
        check_vma=False,
    )
```

profile of v0, /device:TPU:0, one launch (start us, length us, event | category | flops | bytes accessed | tf_op | source)
XLA Modules:
  0.0 131.1 jit_solution(15639445796376129961)
XLA Ops:
  0.0 9.2 %shard_map.91 = f32[640,512]{1,0:T(8,128)} custom-call(bf16[512,2048]{1,0:T(8,128)(2,1)} %bitcast.28, bf16[128,2048]{1,0:T(8,128)(2,1)} %bitcast.31, bf16[2048,256]{1,0:T(8,128)(2,1)} %bi.1, bf16[512,7168]{1,0:T(8,128)(2,1)} %bitcast.12, bf16[128,7168]{1,0:T(8,128)(2,1)} %bitcast.20, bf16[7168,256]{1,0:T(8,128)(2,1)} %refs_0_.4), custom_call_target="tpu_custom_call" | custom-call | flops 3019898880 | bytes 16515072 | tf_op jit(solution)/shard_map/pallas_call | solution.py:71
  9.5 2.6 %collective-permute-start.2 = (bf16[1024,256]{1,0:T(8,128)(2,1)S(1)}, bf16[1024,256]{1,0:T(8,128)(2,1)S(1)}, u32[]{:S(2)}, u32[]{:S(2)}) collective-permute-start(bf16[1024,256]{1,0:T(8,128)(2,1)S(1)} %constant_dynamic-slice_fusion), channel_id=1, source_target_pairs={{0,4},{4,0},{1,5},{5,1},{2,6},{6,2},{3,7},{7,3},{8,12},{12,8},{9,1... | collective-permute-start | bytes 1572872 | tf_op jit(solution)/shard_map/ppermute | solution.py:21
  14.0 2.4 %shard_map.94 = bf16[1024,256]{1,0:T(8,128)(2,1)} custom-call(s32[6]{0:T(128)} %stack.21.where_ref, bf16[7168,256]{1,0:T(8,128)(2,1)} %refs_0_.4), custom_call_target="tpu_custom_call" | custom-call | tf_op jit(solution)/shard_map/pallas_call | solution.py:35
  16.4 3.0 %shard_map.93 = (bf16[1024,256]{1,0:T(8,128)(2,1)}, bf16[1024,256]{1,0:T(8,128)(2,1)}, bf16[1024,256]{1,0:T(8,128)(2,1)}) custom-call(s32[6]{0:T(128)} %stack.21.where_ref, bf16[7168,256]{1,0:T(8,128)(2,1)} %refs_0_.4, bf16[7168,256]{1,0:T(8,128)(2,1)} %refs_0_.4, bf16[7168,256]{1,0:T(8,128)(2,1)} %refs_0_.4), custom_call_target="tpu_custom_call" | custom-call | tf_op jit(solution)/shard_map/pallas_call | solution.py:35
  19.4 2.0 %collective-permute-start.9 = (bf16[1024,256]{1,0:T(8,128)(2,1)}, bf16[1024,256]{1,0:T(8,128)(2,1)}, u32[]{:S(2)}, u32[]{:S(2)}) collective-permute-start(bf16[1024,256]{1,0:T(8,128)(2,1)} %get-tuple-element.18), channel_id=1, source_target_pairs={{0,4},{4,0},{1,5},{5,1},{2,6},{6,2},{3,7},{7,3},{8,12},{12,8},{9,1... | collective-permute-start | bytes 1572872 | tf_op jit(solution)/shard_map/ppermute | solution.py:21
  21.4 3.4 %collective-permute-done.2.refs_4_ = bf16[1024,256]{1,0:T(8,128)(2,1)S(1)} collective-permute-done((bf16[1024,256]{1,0:T(8,128)(2,1)S(1)}, bf16[1024,256]{1,0:T(8,128)(2,1)S(1)}, u32[]{:S(2)}, u32[]{:S(2)}) %collective-permute-start.2) | collective-permute-done | bytes 524320 | tf_op jit(solution)/shard_map/ppermute | solution.py:21
  24.8 2.1 %collective-permute-start.3 = (bf16[1024,256]{1,0:T(8,128)(2,1)S(1)}, bf16[1024,256]{1,0:T(8,128)(2,1)S(1)}, u32[]{:S(2)}, u32[]{:S(2)}) collective-permute-start(bf16[1024,256]{1,0:T(8,128)(2,1)S(1)} %collective-permute-done.2.refs_4_), channel_id=1, source_target_pairs={{0,8},{8,0},{16,24},{24,16},{1,9},{9,1},{17,25},{25,17},{2,10},{10... | collective-permute-start | bytes 1572872 | tf_op jit(solution)/shard_map/ppermute | solution.py:21
  26.9 1.5 %collective-permute-start.6 = (bf16[1024,256]{1,0:T(8,128)(2,1)}, bf16[1024,256]{1,0:T(8,128)(2,1)}, u32[]{:S(2)}, u32[]{:S(2)}) collective-permute-start(bf16[1024,256]{1,0:T(8,128)(2,1)} %get-tuple-element.16), channel_id=1, source_target_pairs={{0,4},{4,0},{1,5},{5,1},{2,6},{6,2},{3,7},{7,3},{8,12},{12,8},{9,1... | collective-permute-start | bytes 1572872 | tf_op jit(solution)/shard_map/ppermute | solution.py:21
  28.4 7.6 %collective-permute-done.11.refs_4_ = bf16[1024,256]{1,0:T(8,128)(2,1)S(1)} collective-permute-done((bf16[1024,256]{1,0:T(8,128)(2,1)}, bf16[1024,256]{1,0:T(8,128)(2,1)S(1)}, u32[]{:S(2)}, u32[]{:S(2)}) %collective-permute-start.11) | collective-permute-done | bytes 524320 | tf_op jit(solution)/shard_map/ppermute | solution.py:21
  36.1 2.1 %collective-permute-start.12 = (bf16[1024,256]{1,0:T(8,128)(2,1)S(1)}, bf16[1024,256]{1,0:T(8,128)(2,1)S(1)}, u32[]{:S(2)}, u32[]{:S(2)}) collective-permute-start(bf16[1024,256]{1,0:T(8,128)(2,1)S(1)} %collective-permute-done.11.refs_4_), channel_id=1, source_target_pairs={{0,8},{8,0},{16,24},{24,16},{1,9},{9,1},{17,25},{25,17},{2,10},{10... | collective-permute-start | bytes 1572872 | tf_op jit(solution)/shard_map/ppermute | solution.py:21
  38.2 9.2 %collective-permute-done.9.refs_4_ = bf16[1024,256]{1,0:T(8,128)(2,1)} collective-permute-done((bf16[1024,256]{1,0:T(8,128)(2,1)}, bf16[1024,256]{1,0:T(8,128)(2,1)}, u32[]{:S(2)}, u32[]{:S(2)}) %collective-permute-start.9) | collective-permute-done | bytes 524320 | tf_op jit(solution)/shard_map/ppermute | solution.py:21
  47.4 2.1 %collective-permute-start.10 = (bf16[1024,256]{1,0:T(8,128)(2,1)}, bf16[1024,256]{1,0:T(8,128)(2,1)}, u32[]{:S(2)}, u32[]{:S(2)}) collective-permute-start(bf16[1024,256]{1,0:T(8,128)(2,1)} %collective-permute-done.9.refs_4_), channel_id=1, source_target_pairs={{0,8},{8,0},{16,24},{24,16},{1,9},{9,1},{17,25},{25,17},{2,10},{10... | collective-permute-start | bytes 1572872 | tf_op jit(solution)/shard_map/ppermute | solution.py:21
  49.5 0.8 copy-done.11
  50.3 4.1 %shard_map.92 = f32[640,256]{1,0:T(8,128)} custom-call(s32[6]{0:T(128)} %stack.21.where_ref, bf16[512,2048]{1,0:T(8,128)(2,1)} %bitcast.29, bf16[512,2048]{1,0:T(8,128)(2,1)} %bitcast.30, bf16[128,2048]{1,0:T(8,128)(2,1)} %bitcast.32, bf16[128,2048]{1,0:T(8,128)(2,1)} %bitcast.33, bf16[1024,256]{1,0:T(8,128)(2,1)} %copy-done.10, bf16[1024,256]{1,0:T(8,128)(2,1)} %copy-done.11), custom_call_target="tpu_custom_call" | custom-call | flops 671088640 | bytes 4980736 | tf_op jit(solution)/shard_map/pallas_call | solution.py:134
  54.4 4.0 %collective-permute-done.6.refs_4_ = bf16[1024,256]{1,0:T(8,128)(2,1)} collective-permute-done((bf16[1024,256]{1,0:T(8,128)(2,1)}, bf16[1024,256]{1,0:T(8,128)(2,1)}, u32[]{:S(2)}, u32[]{:S(2)}) %collective-permute-start.6) | collective-permute-done | bytes 524320 | tf_op jit(solution)/shard_map/ppermute | solution.py:21
  58.5 1.7 %collective-permute-start.8 = (bf16[1024,256]{1,0:T(8,128)(2,1)}, bf16[1024,256]{1,0:T(8,128)(2,1)}, u32[]{:S(2)}, u32[]{:S(2)}) collective-permute-start(bf16[1024,256]{1,0:T(8,128)(2,1)} %get-tuple-element.17), channel_id=1, source_target_pairs={{0,4},{4,0},{1,5},{5,1},{2,6},{6,2},{3,7},{7,3},{8,12},{12,8},{9,1... | collective-permute-start | bytes 1572872 | tf_op jit(solution)/shard_map/ppermute | solution.py:21
  60.2 1.6 %collective-permute-start.7 = (bf16[1024,256]{1,0:T(8,128)(2,1)}, bf16[1024,256]{1,0:T(8,128)(2,1)}, u32[]{:S(2)}, u32[]{:S(2)}) collective-permute-start(bf16[1024,256]{1,0:T(8,128)(2,1)} %collective-permute-done.6.refs_4_), channel_id=1, source_target_pairs={{0,8},{8,0},{16,24},{24,16},{1,9},{9,1},{17,25},{25,17},{2,10},{10... | collective-permute-start | bytes 1572872 | tf_op jit(solution)/shard_map/ppermute | solution.py:21
  61.9 4.1 %shard_map.95.refs_6_ = f32[640,256]{1,0:T(8,128)} custom-call(s32[6]{0:T(128)} %stack.21.where_ref, bf16[512,7168]{1,0:T(8,128)(2,1)} %bitcast.13, bf16[512,7168]{1,0:T(8,128)(2,1)} %bitcast.14, bf16[128,7168]{1,0:T(8,128)(2,1)} %bitcast.21, bf16[128,7168]{1,0:T(8,128)(2,1)} %bitcast.22, bf16[1024,256]{1,0:T(8,128)(2,1)} %copy-done.8, ...), custom_call_target="tpu_custom_call" | custom-call | flops 671088640 | bytes 4980736 | tf_op jit(solution)/shard_map/pallas_call | solution.py:134
  66.0 1.6 %fusion.3 = (bf16[640,512]{1,0:T(8,128)(2,1)S(1)}, f32[640,512]{1,0:T(8,128)S(1)}) fusion(f32[640,512]{1,0:T(8,128)S(1)} %copy-done.1, f32[640,512]{1,0:T(8,128)} %collective-permute-done), kind=kLoop, calls=%fused_computation.11 | loop fusion | flops 655360 | bytes 4587520 | tf_op jit(solution)/shard_map/convert_element_type | solution.py:297
  67.7 1.6 %collective-permute-start.1 = (bf16[640,512]{1,0:T(8,128)(2,1)S(1)}, bf16[640,512]{1,0:T(8,128)(2,1)S(1)}, u32[]{:S(2)}, u32[]{:S(2)}) collective-permute-start(bf16[640,512]{1,0:T(8,128)(2,1)S(1)} %get-tuple-element.31), channel_id=1, source_target_pairs={{0,2},{1,3},{2,0},{3,1},{4,6},{5,7},{6,4},{7,5},{8,10},{9,11},{10,... | collective-permute-start | bytes 1966088 | tf_op jit(solution)/shard_map/ppermute | solution.py:21
  69.3 4.5 %shard_map.96.refs_6_ = f32[640,256]{1,0:T(8,128)} custom-call(s32[6]{0:T(128)} %stack.21.where_ref, bf16[512,7168]{1,0:T(8,128)(2,1)} %bitcast.15, bf16[512,7168]{1,0:T(8,128)(2,1)} %bitcast.16, bf16[128,7168]{1,0:T(8,128)(2,1)} %bitcast.23, bf16[128,7168]{1,0:T(8,128)(2,1)} %bitcast.24, bf16[1024,256]{1,0:T(8,128)(2,1)} %collective-permute-done.9.refs_4_, ...), custom_call_target="tpu_custom_call" | custom-call | flops 671088640 | bytes 4980736 | tf_op jit(solution)/shard_map/pallas_call | solution.py:134
  73.8 4.5 %shard_map.97.refs_3_ = f32[640,256]{1,0:T(8,128)} custom-call(s32[6]{0:T(128)} %stack.21.where_ref, bf16[512,7168]{1,0:T(8,128)(2,1)} %bitcast.17, bf16[512,7168]{1,0:T(8,128)(2,1)} %bitcast.18, bf16[128,7168]{1,0:T(8,128)(2,1)} %bitcast.25, bf16[128,7168]{1,0:T(8,128)(2,1)} %bitcast.26, bf16[1024,256]{1,0:T(8,128)(2,1)} %collective-permute-done.6.refs_4_, ...), custom_call_target="tpu_custom_call" | custom-call | flops 671088640 | bytes 4980736 | tf_op jit(solution)/shard_map/pallas_call | solution.py:134
  78.4 3.9 %shard_map.98 = (f32[512,256]{1,0:T(8,128)}, f32[32,256]{1,0:T(8,128)}, f32[32,256]{1,0:T(8,128)}, f32[32,256]{1,0:T(8,128)}, f32[32,256]{1,0:T(8,128)}) custom-call(s32[6]{0:T(128)} %stack.21.where_ref, bf16[512,7168]{1,0:T(8,128)(2,1)} %bitcast.19, bf16[128,7168]{1,0:T(8,128)(2,1)} %bitcast.27, bf16[1024,256]{1,0:T(8,128)(2,1)} %collective-permute-done.7.refs_2_, ...), custom_call_target="tpu_custom_call" | custom-call | flops 335544320 | bytes 3145728 | tf_op jit(solution)/shard_map/pallas_call | solution.py:134
  83.1 1.1 collective-permute-start.24
  84.2 1.2 fusion.2
  86.0 1.0 collective-permute-done.23
  87.2 1.2 collective-permute-start.25
  88.4 2.6 %collective-permute-start.26 = (bf16[1,32,256]{2,1,0:T(8,128)(2,1)S(1)}, bf16[1,32,256]{2,1,0:T(8,128)(2,1)S(1)}, u32[]{:S(2)}, u32[]{:S(2)}) collective-permute-start(bf16[1,32,256]{2,1,0:T(8,128)(2,1)S(1)} %fusion), channel_id=1, source_target_pairs={{0,16},{8,24},{16,0},{24,8},{1,17},{9,25},{17,1},{25,9},{2,18},{10... | collective-permute-start | bytes 49160 | tf_op jit(solution)/shard_map/ppermute | solution.py:21
  91.0 4.7 %collective-permute-done.5.in_b = bf16[640,256]{1,0:T(8,128)(2,1)S(1)} collective-permute-done((bf16[640,256]{1,0:T(8,128)(2,1)S(1)}, bf16[640,256]{1,0:T(8,128)(2,1)S(1)}, u32[]{:S(2)}, u32[]{:S(2)}) %collective-permute-start.5) | collective-permute-done | bytes 327712 | tf_op jit(solution)/shard_map/ppermute | solution.py:21
  95.7 0.8 collective-permute-start.15
  96.5 2.6 %collective-permute-start.16 = (bf16[1,32,768]{2,1,0:T(8,128)(2,1)S(1)}, bf16[1,32,768]{2,1,0:T(8,128)(2,1)S(1)}, u32[]{:S(2)}, u32[]{:S(2)}) collective-permute-start(bf16[1,32,768]{2,1,0:T(8,128)(2,1)S(1)} %maximum_bitcast_fusion), channel_id=1, source_target_pairs={{0,16},{8,24},{16,0},{24,8},{1,17},{9,25},{17,1},{25,9},{2,18},{10... | collective-permute-start | bytes 147464 | tf_op jit(solution)/shard_map/ppermute | solution.py:21
  99.1 1.1 collective-permute-start.17
  100.2 0.9 fusion.1
  101.1 0.7 collective-permute-start.20
  101.8 3.6 %collective-permute-start.27 = (bf16[1,32,256]{2,1,0:T(8,128)(2,1)S(1)}, bf16[1,32,256]{2,1,0:T(8,128)(2,1)S(1)}, u32[]{:S(2)}, u32[]{:S(2)}) collective-permute-start(bf16[1,32,256]{2,1,0:T(8,128)(2,1)S(1)} %fusion), channel_id=1, source_target_pairs={{0,24},{8,16},{16,8},{24,0},{1,25},{9,17},{17,9},{25,1},{2,26},{10... | collective-permute-start | bytes 49160 | tf_op jit(solution)/shard_map/ppermute | solution.py:21
  106.0 1.3 %collective-permute-done.27 = bf16[1,32,256]{2,1,0:T(8,128)(2,1)S(1)} collective-permute-done((bf16[1,32,256]{2,1,0:T(8,128)(2,1)S(1)}, bf16[1,32,256]{2,1,0:T(8,128)(2,1)S(1)}, u32[]{:S(2)}, u32[]{:S(2)}) %collective-permute-start.27) | collective-permute-done | bytes 16416 | tf_op jit(solution)/shard_map/ppermute | solution.py:21
  107.4 1.0 collective-permute-start.18
  108.5 1.0 collective-permute-start.28
  109.5 0.6 collective-permute-done.20.refs_2_
  110.1 3.1 %collective-permute-done.21.refs_3_ = f32[128,512]{1,0:T(8,128)S(1)} collective-permute-done((f32[128,512]{1,0:T(8,128)S(1)}, f32[128,512]{1,0:T(8,128)S(1)}, u32[]{:S(2)}, u32[]{:S(2)}) %collective-permute-start.21) | collective-permute-done | bytes 262176 | tf_op jit(solution)/shard_map/ppermute | solution.py:21
  113.3 5.4 %collective-permute-done.14.out_b = bf16[512,256]{1,0:T(8,128)(2,1)S(1)} collective-permute-done((bf16[512,256]{1,0:T(8,128)(2,1)S(1)}, bf16[512,256]{1,0:T(8,128)(2,1)S(1)}, u32[]{:S(2)}, u32[]{:S(2)}) %collective-permute-start.14) | collective-permute-done | bytes 262176 | tf_op jit(solution)/shard_map/ppermute | solution.py:21
  118.7 0.7 copy-done.17
  119.5 4.1 %shard_map.99 = (f32[128,256]{1,0:T(8,128)}, f32[128,256]{1,0:T(8,128)}, f32[8,256]{1,0:T(8,128)}) custom-call(s32[6]{0:T(128)} %stack.21.where_ref, f32[640,512]{1,0:T(8,128)} %copy-done, bf16[640,512]{1,0:T(8,128)(2,1)} %copy-done.6, f32[640,256]{1,0:T(8,128)} %copy-done.2, bf16[640,256]{1,0:T(8,128)(2,1)} %copy-done.12, ...), custom_call_target="tpu_custom_call" | custom-call | tf_op jit(solution)/shard_map/pallas_call | solution.py:209
  124.2 1.7 %shard_map.100 = f32[8,128]{1,0:T(8,128)} custom-call(s32[6]{0:T(128)} %stack.21.where_ref, f32[128,256]{1,0:T(8,128)} %get-tuple-element.20.far_ref, f32[128,256]{1,0:T(8,128)} %get-tuple-element.21.near_ref, f32[8,256]{1,0:T(8,128)} %get-tuple-element.22.part_ref, bf16[4,32,256]{2,1,0:T(8,128)(2,1)} %copy-done.13, bf16[4,32,256]{2,1,0:T(8,128)(2,1)} %copy-done.19), custom_call_target="tpu_custom_call" | custom-call | tf_op jit(solution)/shard_map/pallas_call | solution.py:244
  125.9 0.7 collective-permute-start.30
  126.6 1.2 collective-permute-start.31
  127.8 2.0 %collective-permute-done.30 = f32[8,128]{1,0:T(8,128)S(1)} collective-permute-done((f32[8,128]{1,0:T(8,128)}, f32[8,128]{1,0:T(8,128)S(1)}, u32[]{:S(2)}, u32[]{:S(2)}) %collective-permute-start.30) | collective-permute-done | bytes 4128 | tf_op jit(solution)/shard_map/ppermute | solution.py:21
  129.9 0.7 add_add_fusion
  (81 shorter events, 4.6 us)
Async XLA Ops:
  0.0 9.5 %copy-start.4 = (bf16[2048,256]{1,0:T(8,128)(2,1)S(1)}, bf16[2048,256]{1,0:T(8,128)(2,1)}, u32[]{:S(2)}) copy-start(bf16[2048,256]{1,0:T(8,128)(2,1)} %bi.1) | copy-start | bytes 3145732
  9.2 56.7 %collective-permute-start = (f32[640,512]{1,0:T(8,128)}, f32[640,512]{1,0:T(8,128)}, u32[]{:S(2)}, u32[]{:S(2)}) collective-permute-start(f32[640,512]{1,0:T(8,128)} %shard_map.91), channel_id=1, source_target_pairs={{0,1},{1,0},{2,3},{3,2},{4,5},{5,4},{6,7},{7,6},{8,9},{9,8},{10,11... | collective-permute-start | bytes 3932168 | tf_op jit(solution)/shard_map/ppermute | solution.py:21
  9.5 15.3 %collective-permute-start.2 = (bf16[1024,256]{1,0:T(8,128)(2,1)S(1)}, bf16[1024,256]{1,0:T(8,128)(2,1)S(1)}, u32[]{:S(2)}, u32[]{:S(2)}) collective-permute-start(bf16[1024,256]{1,0:T(8,128)(2,1)S(1)} %constant_dynamic-slice_fusion), channel_id=1, source_target_pairs={{0,4},{4,0},{1,5},{5,1},{2,6},{6,2},{3,7},{7,3},{8,12},{12,8},{9,1... | collective-permute-start | bytes 1572872 | tf_op jit(solution)/shard_map/ppermute | solution.py:21
  16.4 19.7 %collective-permute-start.11 = (bf16[1024,256]{1,0:T(8,128)(2,1)}, bf16[1024,256]{1,0:T(8,128)(2,1)S(1)}, u32[]{:S(2)}, u32[]{:S(2)}) collective-permute-start(bf16[1024,256]{1,0:T(8,128)(2,1)} %shard_map.94), channel_id=1, source_target_pairs={{0,4},{4,0},{1,5},{5,1},{2,6},{6,2},{3,7},{7,3},{8,12},{12,8},{9,1... | collective-permute-start | bytes 1572872 | tf_op jit(solution)/shard_map/ppermute | solution.py:21
  19.4 28.0 %collective-permute-start.9 = (bf16[1024,256]{1,0:T(8,128)(2,1)}, bf16[1024,256]{1,0:T(8,128)(2,1)}, u32[]{:S(2)}, u32[]{:S(2)}) collective-permute-start(bf16[1024,256]{1,0:T(8,128)(2,1)} %get-tuple-element.18), channel_id=1, source_target_pairs={{0,4},{4,0},{1,5},{5,1},{2,6},{6,2},{3,7},{7,3},{8,12},{12,8},{9,1... | collective-permute-start | bytes 1572872 | tf_op jit(solution)/shard_map/ppermute | solution.py:21
  24.8 24.7 %copy-start.10 = (bf16[1024,256]{1,0:T(8,128)(2,1)}, bf16[1024,256]{1,0:T(8,128)(2,1)S(1)}, u32[]{:S(2)}) copy-start(bf16[1024,256]{1,0:T(8,128)(2,1)S(1)} %collective-permute-done.2.refs_4_) | copy-start | bytes 1572868
  24.8 24.7 %collective-permute-start.3 = (bf16[1024,256]{1,0:T(8,128)(2,1)S(1)}, bf16[1024,256]{1,0:T(8,128)(2,1)S(1)}, u32[]{:S(2)}, u32[]{:S(2)}) collective-permute-start(bf16[1024,256]{1,0:T(8,128)(2,1)S(1)} %collective-permute-done.2.refs_4_), channel_id=1, source_target_pairs={{0,8},{8,0},{16,24},{24,16},{1,9},{9,1},{17,25},{25,17},{2,10},{10... | collective-permute-start | bytes 1572872 | tf_op jit(solution)/shard_map/ppermute | solution.py:21
  26.9 31.5 %collective-permute-start.6 = (bf16[1024,256]{1,0:T(8,128)(2,1)}, bf16[1024,256]{1,0:T(8,128)(2,1)}, u32[]{:S(2)}, u32[]{:S(2)}) collective-permute-start(bf16[1024,256]{1,0:T(8,128)(2,1)} %get-tuple-element.16), channel_id=1, source_target_pairs={{0,4},{4,0},{1,5},{5,1},{2,6},{6,2},{3,7},{7,3},{8,12},{12,8},{9,1... | collective-permute-start | bytes 1572872 | tf_op jit(solution)/shard_map/ppermute | solution.py:21
  36.1 18.3 %copy-start.8 = (bf16[1024,256]{1,0:T(8,128)(2,1)}, bf16[1024,256]{1,0:T(8,128)(2,1)S(1)}, u32[]{:S(2)}) copy-start(bf16[1024,256]{1,0:T(8,128)(2,1)S(1)} %collective-permute-done.11.refs_4_) | copy-start | bytes 1572868
  36.1 24.1 %collective-permute-start.12 = (bf16[1024,256]{1,0:T(8,128)(2,1)S(1)}, bf16[1024,256]{1,0:T(8,128)(2,1)S(1)}, u32[]{:S(2)}, u32[]{:S(2)}) collective-permute-start(bf16[1024,256]{1,0:T(8,128)(2,1)S(1)} %collective-permute-done.11.refs_4_), channel_id=1, source_target_pairs={{0,8},{8,0},{16,24},{24,16},{1,9},{9,1},{17,25},{25,17},{2,10},{10... | collective-permute-start | bytes 1572872 | tf_op jit(solution)/shard_map/ppermute | solution.py:21
  47.4 20.3 %collective-permute-start.10 = (bf16[1024,256]{1,0:T(8,128)(2,1)}, bf16[1024,256]{1,0:T(8,128)(2,1)}, u32[]{:S(2)}, u32[]{:S(2)}) collective-permute-start(bf16[1024,256]{1,0:T(8,128)(2,1)} %collective-permute-done.9.refs_4_), channel_id=1, source_target_pairs={{0,8},{8,0},{16,24},{24,16},{1,9},{9,1},{17,25},{25,17},{2,10},{10... | collective-permute-start | bytes 1572872 | tf_op jit(solution)/shard_map/ppermute | solution.py:21
  54.4 28.7 %collective-permute-start.4 = (f32[640,256]{1,0:T(8,128)}, f32[640,256]{1,0:T(8,128)}, u32[]{:S(2)}, u32[]{:S(2)}) collective-permute-start(f32[640,256]{1,0:T(8,128)} %shard_map.92), channel_id=1, source_target_pairs={{0,1},{1,0},{2,3},{3,2},{4,5},{5,4},{6,7},{7,6},{8,9},{9,8},{10,11... | collective-permute-start | bytes 1966088 | tf_op jit(solution)/shard_map/ppermute | solution.py:21
  58.5 15.4 %collective-permute-start.8 = (bf16[1024,256]{1,0:T(8,128)(2,1)}, bf16[1024,256]{1,0:T(8,128)(2,1)}, u32[]{:S(2)}, u32[]{:S(2)}) collective-permute-start(bf16[1024,256]{1,0:T(8,128)(2,1)} %get-tuple-element.17), channel_id=1, source_target_pairs={{0,4},{4,0},{1,5},{5,1},{2,6},{6,2},{3,7},{7,3},{8,12},{12,8},{9,1... | collective-permute-start | bytes 1572872 | tf_op jit(solution)/shard_map/ppermute | solution.py:21
  60.2 5.8 %copy-start.14 = (f32[128,512]{1,0:T(8,128)S(1)}, f32[128,512]{1,0:T(8,128)}, u32[]{:S(2)}) copy-start(f32[128,512]{1,0:T(8,128)} %refs_0_.5) | copy-start | bytes 786436
  60.2 5.8 %copy-start.1 = (f32[640,512]{1,0:T(8,128)S(1)}, f32[640,512]{1,0:T(8,128)}, u32[]{:S(2)}) copy-start(f32[640,512]{1,0:T(8,128)} %shard_map.91) | copy-start | bytes 3932164
  60.2 18.2 %collective-permute-start.7 = (bf16[1024,256]{1,0:T(8,128)(2,1)}, bf16[1024,256]{1,0:T(8,128)(2,1)}, u32[]{:S(2)}, u32[]{:S(2)}) collective-permute-start(bf16[1024,256]{1,0:T(8,128)(2,1)} %collective-permute-done.6.refs_4_), channel_id=1, source_target_pairs={{0,8},{8,0},{16,24},{24,16},{1,9},{9,1},{17,25},{25,17},{2,10},{10... | collective-permute-start | bytes 1572872 | tf_op jit(solution)/shard_map/ppermute | solution.py:21
  66.0 42.5 %collective-permute-start.19 = (f32[128,512]{1,0:T(8,128)S(1)}, f32[128,512]{1,0:T(8,128)}, u32[]{:S(2)}, u32[]{:S(2)}) collective-permute-start(f32[128,512]{1,0:T(8,128)S(1)} %copy-done.14), channel_id=1, source_target_pairs={{0,1},{1,0},{2,3},{3,2},{4,5},{5,4},{6,7},{7,6},{8,9},{9,8},{10,11... | collective-permute-start | bytes 786440 | tf_op jit(solution)/shard_map/ppermute | solution.py:21
  67.7 23.3 %copy-start = (f32[640,512]{1,0:T(8,128)}, f32[640,512]{1,0:T(8,128)S(1)}, u32[]{:S(2)}) copy-start(f32[640,512]{1,0:T(8,128)S(1)} %get-tuple-element.32.own_a) | copy-start | bytes 3932164
  67.7 20.7 %collective-permute-start.1 = (bf16[640,512]{1,0:T(8,128)(2,1)S(1)}, bf16[640,512]{1,0:T(8,128)(2,1)S(1)}, u32[]{:S(2)}, u32[]{:S(2)}) collective-permute-start(bf16[640,512]{1,0:T(8,128)(2,1)S(1)} %get-tuple-element.31), channel_id=1, source_target_pairs={{0,2},{1,3},{2,0},{3,1},{4,6},{5,7},{6,4},{7,5},{8,10},{9,11},{10,... | collective-permute-start | bytes 1966088 | tf_op jit(solution)/shard_map/ppermute | solution.py:21
  78.4 5.9 %copy-start.3 = (f32[640,256]{1,0:T(8,128)S(1)}, f32[640,256]{1,0:T(8,128)}, u32[]{:S(2)}) copy-start(f32[640,256]{1,0:T(8,128)} %shard_map.92) | copy-start | bytes 1966084
  82.3 3.1 %copy-start.7 = (f32[512,256]{1,0:T(8,128)S(1)}, f32[512,256]{1,0:T(8,128)}, u32[]{:S(2)}) copy-start(f32[512,256]{1,0:T(8,128)} %get-tuple-element.19) | copy-start | bytes 1572868
  82.3 4.9 %copy-start.20 = (f32[32,256]{1,0:T(8,128)S(1)}, f32[32,256]{1,0:T(8,128)}, u32[]{:S(2)}) copy-start(f32[32,256]{1,0:T(8,128)} %get-tuple-element.23) | copy-start | bytes 98308
  82.3 3.1 %collective-permute-start.22 = (f32[32,256]{1,0:T(8,128)}, f32[32,256]{1,0:T(8,128)S(1)}, u32[]{:S(2)}, u32[]{:S(2)}) collective-permute-start(f32[32,256]{1,0:T(8,128)} %get-tuple-element.24), channel_id=1, source_target_pairs={{0,1},{1,0},{2,3},{3,2},{4,5},{5,4},{6,7},{7,6},{8,9},{9,8},{10,11... | collective-permute-start | bytes 98312 | tf_op jit(solution)/shard_map/ppermute | solution.py:21
  82.6 4.4 %collective-permute-start.23 = (f32[32,256]{1,0:T(8,128)}, f32[32,256]{1,0:T(8,128)S(1)}, u32[]{:S(2)}, u32[]{:S(2)}) collective-permute-start(f32[32,256]{1,0:T(8,128)} %get-tuple-element.25), channel_id=1, source_target_pairs={{0,2},{1,3},{2,0},{3,1},{4,6},{5,7},{6,4},{7,5},{8,10},{9,11},{10,... | collective-permute-start | bytes 98312 | tf_op jit(solution)/shard_map/ppermute | solution.py:21
  83.1 4.1 %collective-permute-start.24 = (f32[32,256]{1,0:T(8,128)}, f32[32,256]{1,0:T(8,128)S(1)}, u32[]{:S(2)}, u32[]{:S(2)}) collective-permute-start(f32[32,256]{1,0:T(8,128)} %get-tuple-element.26), channel_id=1, source_target_pairs={{0,3},{1,2},{2,1},{3,0},{4,7},{5,6},{6,5},{7,4},{8,11},{9,10},{10,... | collective-permute-start | bytes 98312 | tf_op jit(solution)/shard_map/ppermute | solution.py:21
  85.4 20.6 %copy-start.2 = (f32[640,256]{1,0:T(8,128)}, f32[640,256]{1,0:T(8,128)S(1)}, u32[]{:S(2)}) copy-start(f32[640,256]{1,0:T(8,128)S(1)} %get-tuple-element.30.in_a) | copy-start | bytes 1966084
  85.4 13.7 %collective-permute-start.13 = (f32[512,256]{1,0:T(8,128)S(1)}, f32[512,256]{1,0:T(8,128)S(1)}, u32[]{:S(2)}, u32[]{:S(2)}) collective-permute-start(f32[512,256]{1,0:T(8,128)S(1)} %copy-done.7), channel_id=1, source_target_pairs={{0,1},{1,0},{2,3},{3,2},{4,5},{5,4},{6,7},{7,6},{8,9},{9,8},{10,11... | collective-permute-start | bytes 1572872 | tf_op jit(solution)/shard_map/ppermute | solution.py:21
  87.0 8.7 %collective-permute-start.5 = (bf16[640,256]{1,0:T(8,128)(2,1)S(1)}, bf16[640,256]{1,0:T(8,128)(2,1)S(1)}, u32[]{:S(2)}, u32[]{:S(2)}) collective-permute-start(bf16[640,256]{1,0:T(8,128)(2,1)S(1)} %get-tuple-element.29), channel_id=1, source_target_pairs={{0,2},{1,3},{2,0},{3,1},{4,6},{5,7},{6,4},{7,5},{8,10},{9,11},{10,... | collective-permute-start | bytes 983048 | tf_op jit(solution)/shard_map/ppermute | solution.py:21
  87.2 9.3 %collective-permute-start.25 = (bf16[1,32,256]{2,1,0:T(8,128)(2,1)S(1)}, bf16[1,32,256]{2,1,0:T(8,128)(2,1)S(1)}, u32[]{:S(2)}, u32[]{:S(2)}) collective-permute-start(bf16[1,32,256]{2,1,0:T(8,128)(2,1)S(1)} %fusion), channel_id=1, source_target_pairs={{0,8},{8,0},{16,24},{24,16},{1,9},{9,1},{17,25},{25,17},{2,10},{10... | collective-permute-start | bytes 49160 | tf_op jit(solution)/shard_map/ppermute | solution.py:21
  88.4 20.0 %copy-start.6 = (bf16[640,512]{1,0:T(8,128)(2,1)}, bf16[640,512]{1,0:T(8,128)(2,1)S(1)}, u32[]{:S(2)}) copy-start(bf16[640,512]{1,0:T(8,128)(2,1)S(1)} %collective-permute-done.1.own_b) | copy-start | bytes 1966084
  88.4 12.7 %collective-permute-start.26 = (bf16[1,32,256]{2,1,0:T(8,128)(2,1)S(1)}, bf16[1,32,256]{2,1,0:T(8,128)(2,1)S(1)}, u32[]{:S(2)}, u32[]{:S(2)}) collective-permute-start(bf16[1,32,256]{2,1,0:T(8,128)(2,1)S(1)} %fusion), channel_id=1, source_target_pairs={{0,16},{8,24},{16,0},{24,8},{1,17},{9,25},{17,1},{25,9},{2,18},{10... | collective-permute-start | bytes 49160 | tf_op jit(solution)/shard_map/ppermute | solution.py:21
  95.7 3.4 %copy-start.12 = (bf16[640,256]{1,0:T(8,128)(2,1)}, bf16[640,256]{1,0:T(8,128)(2,1)S(1)}, u32[]{:S(2)}) copy-start(bf16[640,256]{1,0:T(8,128)(2,1)S(1)} %collective-permute-done.5.in_b) | copy-start | bytes 983044
  95.7 6.0 %collective-permute-start.15 = (bf16[1,32,768]{2,1,0:T(8,128)(2,1)S(1)}, bf16[1,32,768]{2,1,0:T(8,128)(2,1)S(1)}, u32[]{:S(2)}, u32[]{:S(2)}) collective-permute-start(bf16[1,32,768]{2,1,0:T(8,128)(2,1)S(1)} %maximum_bitcast_fusion), channel_id=1, source_target_pairs={{0,8},{8,0},{16,24},{24,16},{1,9},{9,1},{17,25},{25,17},{2,10},{10... | collective-permute-start | bytes 147464 | tf_op jit(solution)/shard_map/ppermute | solution.py:21
  96.5 5.2 %collective-permute-start.16 = (bf16[1,32,768]{2,1,0:T(8,128)(2,1)S(1)}, bf16[1,32,768]{2,1,0:T(8,128)(2,1)S(1)}, u32[]{:S(2)}, u32[]{:S(2)}) collective-permute-start(bf16[1,32,768]{2,1,0:T(8,128)(2,1)S(1)} %maximum_bitcast_fusion), channel_id=1, source_target_pairs={{0,16},{8,24},{16,0},{24,8},{1,17},{9,25},{17,1},{25,9},{2,18},{10... | collective-permute-start | bytes 147464 | tf_op jit(solution)/shard_map/ppermute | solution.py:21
  99.1 6.2 %collective-permute-start.17 = (bf16[1,32,768]{2,1,0:T(8,128)(2,1)S(1)}, bf16[1,32,768]{2,1,0:T(8,128)(2,1)S(1)}, u32[]{:S(2)}, u32[]{:S(2)}) collective-permute-start(bf16[1,32,768]{2,1,0:T(8,128)(2,1)S(1)} %maximum_bitcast_fusion), channel_id=1, source_target_pairs={{0,24},{8,16},{16,8},{24,0},{1,25},{9,17},{17,9},{25,1},{2,26},{10... | collective-permute-start | bytes 147464 | tf_op jit(solution)/shard_map/ppermute | solution.py:21
  101.1 9.1 %collective-permute-start.20 = (f32[128,512]{1,0:T(8,128)S(1)}, f32[128,512]{1,0:T(8,128)S(1)}, u32[]{:S(2)}, u32[]{:S(2)}) collective-permute-start(f32[128,512]{1,0:T(8,128)S(1)} %copy-done.14), channel_id=1, source_target_pairs={{0,2},{1,3},{2,0},{3,1},{4,6},{5,7},{6,4},{7,5},{8,10},{9,11},{10,... | collective-permute-start | bytes 786440 | tf_op jit(solution)/shard_map/ppermute | solution.py:21
  101.7 11.5 %collective-permute-start.21 = (f32[128,512]{1,0:T(8,128)S(1)}, f32[128,512]{1,0:T(8,128)S(1)}, u32[]{:S(2)}, u32[]{:S(2)}) collective-permute-start(f32[128,512]{1,0:T(8,128)S(1)} %copy-done.14), channel_id=1, source_target_pairs={{0,3},{1,2},{2,1},{3,0},{4,7},{5,6},{6,5},{7,4},{8,11},{9,10},{10,... | collective-permute-start | bytes 786440 | tf_op jit(solution)/shard_map/ppermute | solution.py:21
  101.8 5.6 %collective-permute-start.27 = (bf16[1,32,256]{2,1,0:T(8,128)(2,1)S(1)}, bf16[1,32,256]{2,1,0:T(8,128)(2,1)S(1)}, u32[]{:S(2)}, u32[]{:S(2)}) collective-permute-start(bf16[1,32,256]{2,1,0:T(8,128)(2,1)S(1)} %fusion), channel_id=1, source_target_pairs={{0,24},{8,16},{16,8},{24,0},{1,25},{9,17},{17,9},{25,1},{2,26},{10... | collective-permute-start | bytes 49160 | tf_op jit(solution)/shard_map/ppermute | solution.py:21
  105.4 13.3 %collective-permute-start.14 = (bf16[512,256]{1,0:T(8,128)(2,1)S(1)}, bf16[512,256]{1,0:T(8,128)(2,1)S(1)}, u32[]{:S(2)}, u32[]{:S(2)}) collective-permute-start(bf16[512,256]{1,0:T(8,128)(2,1)S(1)} %get-tuple-element.27), channel_id=1, source_target_pairs={{0,2},{1,3},{2,0},{3,1},{4,6},{5,7},{6,4},{7,5},{8,10},{9,11},{10,... | collective-permute-start | bytes 786440 | tf_op jit(solution)/shard_map/ppermute | solution.py:21
  106.0 12.7 %copy-start.5 = (bf16[4,32,768]{2,1,0:T(8,128)(2,1)}, bf16[4,32,768]{2,1,0:T(8,128)(2,1)S(1)}, u32[]{:S(2)}) copy-start(bf16[4,32,768]{2,1,0:T(8,128)(2,1)S(1)} %pad_maximum_fusion.qa) | copy-start | bytes 589828
  107.4 11.3 %collective-permute-start.18 = (bf16[4,32,768]{2,1,0:T(8,128)(2,1)S(1)}, bf16[4,32,768]{2,1,0:T(8,128)(2,1)S(1)}, u32[]{:S(2)}, u32[]{:S(2)}) collective-permute-start(bf16[4,32,768]{2,1,0:T(8,128)(2,1)S(1)} %pad_maximum_fusion.qa), channel_id=1, source_target_pairs={{0,4},{4,0},{1,5},{5,1},{2,6},{6,2},{3,7},{7,3},{8,12},{12,8},{9,1... | collective-permute-start | bytes 589832 | tf_op jit(solution)/shard_map/ppermute | solution.py:21
  108.4 15.1 %copy-start.13 = (bf16[4,32,256]{2,1,0:T(8,128)(2,1)}, bf16[4,32,256]{2,1,0:T(8,128)(2,1)S(1)}, u32[]{:S(2)}) copy-start(bf16[4,32,256]{2,1,0:T(8,128)(2,1)S(1)} %pad_maximum_fusion.1.la) | copy-start | bytes 196612
  108.5 15.1 %collective-permute-start.28 = (bf16[4,32,256]{2,1,0:T(8,128)(2,1)S(1)}, bf16[4,32,256]{2,1,0:T(8,128)(2,1)S(1)}, u32[]{:S(2)}, u32[]{:S(2)}) collective-permute-start(bf16[4,32,256]{2,1,0:T(8,128)(2,1)S(1)} %pad_maximum_fusion.1.la), channel_id=1, source_target_pairs={{0,4},{4,0},{1,5},{5,1},{2,6},{6,2},{3,7},{7,3},{8,12},{12,8},{9,1... | collective-permute-start | bytes 196616 | tf_op jit(solution)/shard_map/ppermute | solution.py:21
  110.1 8.6 %copy-start.15 = (f32[128,512]{1,0:T(8,128)}, f32[128,512]{1,0:T(8,128)S(1)}, u32[]{:S(2)}) copy-start(f32[128,512]{1,0:T(8,128)S(1)} %collective-permute-done.20.refs_2_) | copy-start | bytes 786436
  113.3 5.4 %copy-start.16 = (f32[128,512]{1,0:T(8,128)}, f32[128,512]{1,0:T(8,128)S(1)}, u32[]{:S(2)}) copy-start(f32[128,512]{1,0:T(8,128)S(1)} %collective-permute-done.21.refs_3_) | copy-start | bytes 786436
  125.9 1.9 %collective-permute-start.29 = (f32[8,128]{1,0:T(8,128)}, f32[8,128]{1,0:T(8,128)S(1)}, u32[]{:S(2)}, u32[]{:S(2)}) collective-permute-start(f32[8,128]{1,0:T(8,128)} %shard_map.100), channel_id=1, source_target_pairs={{0,1},{1,0},{2,3},{3,2},{4,5},{5,4},{6,7},{7,6},{8,9},{9,8},{10,11... | collective-permute-start | bytes 12296 | tf_op jit(solution)/shard_map/ppermute | solution.py:21
  125.9 3.8 %collective-permute-start.30 = (f32[8,128]{1,0:T(8,128)}, f32[8,128]{1,0:T(8,128)S(1)}, u32[]{:S(2)}, u32[]{:S(2)}) collective-permute-start(f32[8,128]{1,0:T(8,128)} %shard_map.100), channel_id=1, source_target_pairs={{0,2},{1,3},{2,0},{3,1},{4,6},{5,7},{6,4},{7,5},{8,10},{9,11},{10,... | collective-permute-start | bytes 12296 | tf_op jit(solution)/shard_map/ppermute | solution.py:21
  126.6 3.2 %collective-permute-start.31 = (f32[8,128]{1,0:T(8,128)}, f32[8,128]{1,0:T(8,128)S(1)}, u32[]{:S(2)}, u32[]{:S(2)}) collective-permute-start(f32[8,128]{1,0:T(8,128)} %shard_map.100), channel_id=1, source_target_pairs={{0,3},{1,2},{2,1},{3,0},{4,7},{5,6},{6,5},{7,4},{8,11},{9,10},{10,... | collective-permute-start | bytes 12296 | tf_op jit(solution)/shard_map/ppermute | solution.py:21
  (5 other events, 4.6 us)
where the time goes:
time: 132 us; the launch traced here: 131 us
  waiting for transfers between devices  42.6 us (32%)
  Pallas kernels  41.6 us (32%)
  starting transfers between devices  37.4 us (28%)
  other arithmetic  4.44 us (3%)
  local copies, waits for them, and re-layouts  3.4 us (3%)
  between operations  1.53 us (1%)
    ppermute x32, waiting for transfers between devices, flip(): return lax.ppermute(array, axis, [(i, i ^ mask) for i in range(size)])  42.6 us
    ppermute x32, starting transfers between devices, flip(): return lax.ppermute(array, axis, [(i, i ^ mask) for i in range(size)])  37.4 us
    pallas_call x5, Pallas kernels, rotate(): pl.pallas_call(body, out_shape=[jax.ShapeDtypeStruct(shape, jnp.float32)...  21.2 us
    pallas_call x1, Pallas kernels, rotate_own(): pl.pallas_call(body, out_shape=jax.ShapeDtypeStruct((total + qtotal, 2 *...  9.22 us
    pallas_call x2, Pallas kernels, cut(): pl.pallas_call(body, out_shape=[jax.ShapeDtypeStruct((size, width), basis...  5.41 us
    pallas_call x1, Pallas kernels, weigh(): pl.pallas_call(body, out_shape=[product, product, jax.ShapeDtypeStruct((2...  4.1 us
    convert_element_type x3, other arithmetic, shared(): return (value, flip(value.astype(bf16), 'tensor', bits[-1]))  3.69 us
  transfers between devices with their start and end apart: 32, of which 12 were waited for; matrix products, arithmetic and copies ran while one was open for 3% of the time, Pallas kernels for 23%

commit v1 on v0

--- a/solution.py
+++ b/solution.py
@@ -150,69 +150,102 @@
     return outs if ways else outs[0]
 
 
-def weigh(where, own, inner, outer, query, corr):
-    length, half = outer[0].shape
+def meet(rows, inputs, curvatures, queries):
+    total = jnp.zeros((queries[0].shape[0], rows.shape[1]), jnp.float32)
+    for given, curvature, query in zip(inputs, curvatures, queries):
+        rot = lax.dot_general(rows, given, (((0,), (0,)), ((), ())), preferred_element_type=jnp.float32)
+        weight = rot.astype(jnp.bfloat16).astype(jnp.float32) * curvature
+        high = weight.astype(jnp.bfloat16)
+        low = (weight - high.astype(jnp.float32)).astype(jnp.bfloat16)
+        for part in (high, low):
+            total += lax.dot_general(
+                query, part, (((1,), (1,)), ((), ())), preferred_element_type=jnp.float32
+            )
+    return total
+
+
+def live_rows(where_ref, shape):
+    position = lax.broadcasted_iota(jnp.int32, shape, 0)
+    return ((position >= where_ref[BEGIN]) & (position < where_ref[END])).astype(jnp.bfloat16)
+
+
+def weigh_own(where, length, own, inner, query, corr):
+    half = inner[0].shape[1]
     places, share, _ = query[0].shape
     rows = places * share
     blocks, tall = len(corr), corr[0].shape[0]
 
-    def body(where_ref, own_a, own_b, in_a, in_b, out_a, out_b, qa, qb, *refs):
-        corr_refs, (far_ref, near_ref, part_ref), curv = refs[:blocks], refs[blocks:-1], refs[-1]
-        side, begin, end = where_ref[OWNER], where_ref[BEGIN], where_ref[END]
+    def body(where_ref, own_a, own_b, in_a, in_b, qa, qb, *refs):
+        corr_refs, (far_ref, part_ref, ins_ref, qins_ref, curv_ref, curv) = refs[:blocks], refs[blocks:]
+        side = where_ref[OWNER]
         for k in range(blocks):
             curv[pl.ds(pl.multiple_of((where_ref[PLACE] ^ k) * tall, tall), tall), :] = corr_refs[k][...]
 
         def rounded(a, b, cols):
             return (a[:length, cols] + b[:length, cols].astype(jnp.float32)).astype(jnp.bfloat16)
 
+        def inverse(i, j):
+            return 1.0 / (
+                curv[
+                    pl.ds(pl.multiple_of((side ^ i) * half, half), half),
+                    pl.ds(pl.multiple_of((side ^ j) * half, half), half),
+                ]
+                + damping
+            )
+
         everything, first, second = slice(None), slice(0, half), slice(half, 2 * half)
         ins = (rounded(own_a, own_b, first), rounded(in_a, in_b, everything))
-        outs = (rounded(own_a, own_b, second), rounded(out_a, out_b, everything))
-        position = lax.broadcasted_iota(jnp.int32, (length, half), 0)
-        live = ((position >= begin) & (position < end)).astype(jnp.bfloat16)
         near = qa[...].reshape(rows, 3 * half)
         far = qb[...].reshape(rows, 3 * half)
         qins = (
             jnp.concatenate([near[:, :half], far[:, 2 * half :]], 0),
             jnp.concatenate([near[:, 2 * half :], far[:, :half]], 0),
         )
-        moved = []
-        for h in range(2):
-            masked = outs[h] * live
-            total = jnp.zeros((2 * rows, half), jnp.float32)
-            for j in range(2):
-                rot = lax.dot_general(
-                    masked, ins[j], (((0,), (0,)), ((), ())), preferred_element_type=jnp.float32
-                )
-                rot = rot.astype(jnp.bfloat16).astype(jnp.float32)
-                weight = rot / (
-                    curv[
-                        pl.ds(pl.multiple_of((side ^ h) * half, half), half),
-                        pl.ds(pl.multiple_of((side ^ j) * half, half), half),
-                    ]
-                    + damping
-                )
-                high = weight.astype(jnp.bfloat16)
-                low = (weight - high.astype(jnp.float32)).astype(jnp.bfloat16)
-                for part in (high, low):
-                    total += lax.dot_general(
-                        qins[j], part, (((1,), (1,)), ((), ())), preferred_element_type=jnp.float32
-                    )
-            moved.append(total)
-        near_ref[...] = moved[1][:rows]
-        far_ref[...] = moved[0][rows:]
-        part_ref[:places, :] = row_sums(moved[0][:rows] * near[:, half : 2 * half].astype(jnp.float32), places)
-        part_ref[places:, :] = row_sums(moved[1][rows:] * far[:, half : 2 * half].astype(jnp.float32), places)
+        masked = rounded(own_a, own_b, second) * live_rows(where_ref, (length, half))
+        total = meet(masked, ins, [inverse(0, 0), inverse(0, 1)], qins)
+        far_ref[...] = total[rows:]
+        part_ref[...] = row_sums(total[:rows] * near[:, half : 2 * half].astype(jnp.float32), places)
+        for j in range(2):
+            ins_ref[j] = ins[j]
+            qins_ref[j] = qins[j]
+            curv_ref[j] = inverse(1, j)
 
     vmem = pl.BlockSpec(memory_space=pltpu.VMEM)
-    product = jax.ShapeDtypeStruct((rows, half), jnp.float32)
     return pl.pallas_call(
         body,
-        out_shape=[product, product, jax.ShapeDtypeStruct((2 * places, half), jnp.float32)],
-        in_specs=[pl.BlockSpec(memory_space=pltpu.SMEM)] + [vmem] * (8 + blocks),
-        out_specs=[vmem] * 3,
+        out_shape=[
+            jax.ShapeDtypeStruct((rows, half), jnp.float32),
+            jax.ShapeDtypeStruct((places, half), jnp.float32),
+            jax.ShapeDtypeStruct((2, length, half), jnp.bfloat16),
+            jax.ShapeDtypeStruct((2, 2 * rows, half), jnp.bfloat16),
+            jax.ShapeDtypeStruct((2, half, half), jnp.float32),
+        ],
+        in_specs=[pl.BlockSpec(memory_space=pltpu.SMEM)] + [vmem] * (6 + blocks),
+        out_specs=[vmem] * 5,
         scratch_shapes=[pltpu.VMEM((blocks * tall, corr[0].shape[1]), jnp.float32)],
-    )(where, *own, *inner, *outer, *query, *corr)
+    )(where, *own, *inner, *query, *corr)
+
+
+def weigh_other(where, outer, ins, qins, curvature, far):
+    length, half = outer[0].shape
+    places, share, _ = far.shape
+    rows = places * share
+
+    def body(where_ref, out_a, out_b, ins_ref, qins_ref, curv_ref, far_ref, near_ref, part_ref):
+        rounded = (out_a[...] + out_b[...].astype(jnp.float32)).astype(jnp.bfloat16)
+        masked = rounded * live_rows(where_ref, (length, half))
+        total = meet(masked, [ins_ref[j] for j in range(2)], [curv_ref[j] for j in range(2)], [qins_ref[j] for j in range(2)])
+        near_ref[...] = total[:rows]
+        theirs = far_ref[...].reshape(rows, 3 * half)[:, half : 2 * half]
+        part_ref[...] = row_sums(total[rows:] * theirs.astype(jnp.float32), places)
+
+    vmem = pl.BlockSpec(memory_space=pltpu.VMEM)
+    return pl.pallas_call(
+        body,
+        out_shape=[jax.ShapeDtypeStruct((rows, half), jnp.float32), jax.ShapeDtypeStruct((places, half), jnp.float32)],
+        in_specs=[pl.BlockSpec(memory_space=pltpu.SMEM)] + [vmem] * 6,
+        out_specs=[vmem] * 2,
+    )(where, *outer, ins, qins, curvature, far)
 
 
 def row_sums(values, places):
@@ -221,15 +254,14 @@
 
 
 def gather_scores(where, moved, late, masks):
-    far, near, part = moved
     places, share, half = late[0].shape
     count = 2 * places
 
-    def body(where_ref, far_ref, near_ref, part_ref, la, lb, out_ref):
+    def body(where_ref, far_ref, part_a, near_ref, part_b, la, lb, out_ref):
         def met(product, block):
             return row_sums(product[...] * block[...].reshape(places * share, half).astype(jnp.float32), places)
 
-        sums = part_ref[...] + jnp.concatenate([met(near_ref, la), met(far_ref, lb)], 0)
+        sums = jnp.concatenate([part_a[...] + met(near_ref, la), part_b[...] + met(far_ref, lb)], 0)
         sums = jnp.sum(sums, axis=1, keepdims=True)
         index = lax.broadcasted_iota(jnp.int32, (count, 128), 0)
         query = jnp.zeros((count, 128), jnp.int32)
@@ -244,9 +276,9 @@
     return pl.pallas_call(
         body,
         out_shape=jax.ShapeDtypeStruct((8, 128), jnp.float32),
-        in_specs=[pl.BlockSpec(memory_space=pltpu.SMEM)] + [vmem] * 5,
+        in_specs=[pl.BlockSpec(memory_space=pltpu.SMEM)] + [vmem] * 6,
         out_specs=vmem,
-    )(where, far, near, part, *late)
+    )(where, *moved, *late)
 
 
 def on_device(
@@ -343,7 +375,9 @@
     late = everyone(qsum.astype(bf16))
     outer = shared(outer)
 
-    moved = weigh(where, own, inner, outer, early, corr)
+    far, own_part, *kept = weigh_own(where, length, own, inner, early, corr)
+    near, other_part = weigh_other(where, outer, *kept, early[1])
+    moved = (far, own_part, near, other_part)
     scores = gather_scores(where, moved, late, masks)
     pieces = [scores]
     for k in range(1, tensor_size):

time: 132 us -> 132 us (level)
  Pallas kernels: 41.6 us -> 44.3 us
  starting transfers between devices: 37.4 us -> 35.4 us
  waiting for transfers between devices: 42.6 us -> 40.6 us
  local copies, waits for them, and re-layouts: 3.4 us -> 4.77 us
    pallas_call x1 -> x2, Pallas kernels: 4.1 us -> 6.82 us  [the longest x1 3.93 us: weigh_own(): pl.pallas_call(body, out_shape=[jax.ShapeDtypeStruct((rows, half), jnp.fl...]
    ppermute x32, starting transfers between devices: 37.4 us -> 35.4 us  [flip(): return lax.ppermute(array, axis, [(i, i ^ mask) for i in range(size)])]
    ppermute x32, waiting for transfers between devices: 42.6 us -> 40.6 us  [flip(): return lax.ppermute(array, axis, [(i, i ^ mask) for i in range(size)])]
  transfers between devices with their start and end apart: 32 -> 32, of which waited for: 12 -> 12; matrix products, arithmetic and copies ran while one was open for 3% -> 3% of each run, Pallas kernels for 23% -> 25%
where the time goes in v1:
time: 132 us; the launch traced here: 131 us
  Pallas kernels  44.3 us (34%)
  waiting for transfers between devices  40.6 us (31%)
  starting transfers between devices  35.4 us (27%)
  local copies, waits for them, and re-layouts  4.77 us (4%)
  other arithmetic  4.45 us (3%)
  between operations  1.53 us (1%)
    ppermute x32, waiting for transfers between devices, flip(): return lax.ppermute(array, axis, [(i, i ^ mask) for i in range(size)])  40.6 us
    ppermute x32, starting transfers between devices, flip(): return lax.ppermute(array, axis, [(i, i ^ mask) for i in range(size)])  35.4 us
    pallas_call x5, Pallas kernels, rotate(): pl.pallas_call(body, out_shape=[jax.ShapeDtypeStruct(shape, jnp.float32)...  21.1 us
    pallas_call x1, Pallas kernels, rotate_own(): pl.pallas_call(body, out_shape=jax.ShapeDtypeStruct((total + qtotal, 2 *...  9.22 us
    pallas_call x2, Pallas kernels, cut(): pl.pallas_call(body, out_shape=[jax.ShapeDtypeStruct((size, width), basis...  5.41 us
    pallas_call x1, Pallas kernels, weigh_own(): pl.pallas_call(body, out_shape=[jax.ShapeDtypeStruct((rows, half), jnp.fl...  3.93 us
    convert_element_type x3, other arithmetic, shared(): return (value, flip(value.astype(bf16), 'tensor', bits[-1]))  3.68 us
    unnamed x42, local copies, waits for them, and re-layouts  3.54 us
  transfers between devices with their start and end apart: 32, of which 12 were waited for; matrix products, arithmetic and copies ran while one was open for 3% of the time, Pallas kernels for 25%

profile of v1, /device:TPU:0, one launch (start us, length us, event | category | flops | bytes accessed | tf_op | source)
XLA Modules:
  0.0 131.1 jit_solution(16127015147077180585)
XLA Ops:
  0.0 9.2 %shard_map.91 = f32[640,512]{1,0:T(8,128)} custom-call(bf16[512,2048]{1,0:T(8,128)(2,1)} %bitcast.28, bf16[128,2048]{1,0:T(8,128)(2,1)} %bitcast.31, bf16[2048,256]{1,0:T(8,128)(2,1)} %bi.1, bf16[512,7168]{1,0:T(8,128)(2,1)} %bitcast.12, bf16[128,7168]{1,0:T(8,128)(2,1)} %bitcast.20, bf16[7168,256]{1,0:T(8,128)(2,1)} %refs_0_.5), custom_call_target="tpu_custom_call" | custom-call | flops 3019898880 | bytes 16515072 | tf_op jit(solution)/shard_map/pallas_call | solution.py:71
  9.5 2.6 %collective-permute-start.2 = (bf16[1024,256]{1,0:T(8,128)(2,1)S(1)}, bf16[1024,256]{1,0:T(8,128)(2,1)S(1)}, u32[]{:S(2)}, u32[]{:S(2)}) collective-permute-start(bf16[1024,256]{1,0:T(8,128)(2,1)S(1)} %constant_dynamic-slice_fusion), channel_id=1, source_target_pairs={{0,4},{4,0},{1,5},{5,1},{2,6},{6,2},{3,7},{7,3},{8,12},{12,8},{9,1... | collective-permute-start | bytes 1572872 | tf_op jit(solution)/shard_map/ppermute | solution.py:21
  13.4 0.7 stack.21.where_ref
  14.0 2.4 %shard_map.95 = bf16[1024,256]{1,0:T(8,128)(2,1)} custom-call(s32[6]{0:T(128)} %stack.21.where_ref, bf16[7168,256]{1,0:T(8,128)(2,1)} %refs_0_.5), custom_call_target="tpu_custom_call" | custom-call | tf_op jit(solution)/shard_map/pallas_call | solution.py:35
  16.5 3.0 %shard_map.94 = (bf16[1024,256]{1,0:T(8,128)(2,1)}, bf16[1024,256]{1,0:T(8,128)(2,1)}, bf16[1024,256]{1,0:T(8,128)(2,1)}) custom-call(s32[6]{0:T(128)} %stack.21.where_ref, bf16[7168,256]{1,0:T(8,128)(2,1)} %refs_0_.5, bf16[7168,256]{1,0:T(8,128)(2,1)} %refs_0_.5, bf16[7168,256]{1,0:T(8,128)(2,1)} %refs_0_.5), custom_call_target="tpu_custom_call" | custom-call | tf_op jit(solution)/shard_map/pallas_call | solution.py:35
  19.5 2.0 %collective-permute-start.16 = (bf16[1024,256]{1,0:T(8,128)(2,1)}, bf16[1024,256]{1,0:T(8,128)(2,1)}, u32[]{:S(2)}, u32[]{:S(2)}) collective-permute-start(bf16[1024,256]{1,0:T(8,128)(2,1)} %get-tuple-element.24), channel_id=1, source_target_pairs={{0,4},{4,0},{1,5},{5,1},{2,6},{6,2},{3,7},{7,3},{8,12},{12,8},{9,1... | collective-permute-start | bytes 1572872 | tf_op jit(solution)/shard_map/ppermute | solution.py:21
  21.5 3.3 %collective-permute-done.2.refs_4_ = bf16[1024,256]{1,0:T(8,128)(2,1)S(1)} collective-permute-done((bf16[1024,256]{1,0:T(8,128)(2,1)S(1)}, bf16[1024,256]{1,0:T(8,128)(2,1)S(1)}, u32[]{:S(2)}, u32[]{:S(2)}) %collective-permute-start.2) | collective-permute-done | bytes 524320 | tf_op jit(solution)/shard_map/ppermute | solution.py:21
  24.8 2.1 %collective-permute-start.3 = (bf16[1024,256]{1,0:T(8,128)(2,1)S(1)}, bf16[1024,256]{1,0:T(8,128)(2,1)S(1)}, u32[]{:S(2)}, u32[]{:S(2)}) collective-permute-start(bf16[1024,256]{1,0:T(8,128)(2,1)S(1)} %collective-permute-done.2.refs_4_), channel_id=1, source_target_pairs={{0,8},{8,0},{16,24},{24,16},{1,9},{9,1},{17,25},{25,17},{2,10},{10... | collective-permute-start | bytes 1572872 | tf_op jit(solution)/shard_map/ppermute | solution.py:21
  26.9 1.5 %collective-permute-start.13 = (bf16[1024,256]{1,0:T(8,128)(2,1)}, bf16[1024,256]{1,0:T(8,128)(2,1)}, u32[]{:S(2)}, u32[]{:S(2)}) collective-permute-start(bf16[1024,256]{1,0:T(8,128)(2,1)} %get-tuple-element.22), channel_id=1, source_target_pairs={{0,4},{4,0},{1,5},{5,1},{2,6},{6,2},{3,7},{7,3},{8,12},{12,8},{9,1... | collective-permute-start | bytes 1572872 | tf_op jit(solution)/shard_map/ppermute | solution.py:21
  28.4 7.6 %collective-permute-done.18.refs_4_ = bf16[1024,256]{1,0:T(8,128)(2,1)S(1)} collective-permute-done((bf16[1024,256]{1,0:T(8,128)(2,1)}, bf16[1024,256]{1,0:T(8,128)(2,1)S(1)}, u32[]{:S(2)}, u32[]{:S(2)}) %collective-permute-start.18) | collective-permute-done | bytes 524320 | tf_op jit(solution)/shard_map/ppermute | solution.py:21
  36.1 2.1 %collective-permute-start.19 = (bf16[1024,256]{1,0:T(8,128)(2,1)S(1)}, bf16[1024,256]{1,0:T(8,128)(2,1)S(1)}, u32[]{:S(2)}, u32[]{:S(2)}) collective-permute-start(bf16[1024,256]{1,0:T(8,128)(2,1)S(1)} %collective-permute-done.18.refs_4_), channel_id=1, source_target_pairs={{0,8},{8,0},{16,24},{24,16},{1,9},{9,1},{17,25},{25,17},{2,10},{10... | collective-permute-start | bytes 1572872 | tf_op jit(solution)/shard_map/ppermute | solution.py:21
  38.2 9.2 %collective-permute-done.16.refs_4_ = bf16[1024,256]{1,0:T(8,128)(2,1)} collective-permute-done((bf16[1024,256]{1,0:T(8,128)(2,1)}, bf16[1024,256]{1,0:T(8,128)(2,1)}, u32[]{:S(2)}, u32[]{:S(2)}) %collective-permute-start.16) | collective-permute-done | bytes 524320 | tf_op jit(solution)/shard_map/ppermute | solution.py:21
  47.4 2.1 %collective-permute-start.17 = (bf16[1024,256]{1,0:T(8,128)(2,1)}, bf16[1024,256]{1,0:T(8,128)(2,1)}, u32[]{:S(2)}, u32[]{:S(2)}) collective-permute-start(bf16[1024,256]{1,0:T(8,128)(2,1)} %collective-permute-done.16.refs_4_), channel_id=1, source_target_pairs={{0,8},{8,0},{16,24},{24,16},{1,9},{9,1},{17,25},{25,17},{2,10},{10... | collective-permute-start | bytes 1572872 | tf_op jit(solution)/shard_map/ppermute | solution.py:21
  49.5 0.8 copy-done.12
  50.3 4.1 %shard_map.92 = f32[640,256]{1,0:T(8,128)} custom-call(s32[6]{0:T(128)} %stack.21.where_ref, bf16[512,2048]{1,0:T(8,128)(2,1)} %bitcast.29, bf16[512,2048]{1,0:T(8,128)(2,1)} %bitcast.30, bf16[128,2048]{1,0:T(8,128)(2,1)} %bitcast.32, bf16[128,2048]{1,0:T(8,128)(2,1)} %bitcast.33, bf16[1024,256]{1,0:T(8,128)(2,1)} %copy-done.11, bf16[1024,256]{1,0:T(8,128)(2,1)} %copy-done.12), custom_call_target="tpu_custom_call" | custom-call | flops 671088640 | bytes 4980736 | tf_op jit(solution)/shard_map/pallas_call | solution.py:134
  54.4 4.0 %collective-permute-done.13.refs_4_ = bf16[1024,256]{1,0:T(8,128)(2,1)} collective-permute-done((bf16[1024,256]{1,0:T(8,128)(2,1)}, bf16[1024,256]{1,0:T(8,128)(2,1)}, u32[]{:S(2)}, u32[]{:S(2)}) %collective-permute-start.13) | collective-permute-done | bytes 524320 | tf_op jit(solution)/shard_map/ppermute | solution.py:21
  58.4 1.7 %collective-permute-start.15 = (bf16[1024,256]{1,0:T(8,128)(2,1)}, bf16[1024,256]{1,0:T(8,128)(2,1)}, u32[]{:S(2)}, u32[]{:S(2)}) collective-permute-start(bf16[1024,256]{1,0:T(8,128)(2,1)} %get-tuple-element.23), channel_id=1, source_target_pairs={{0,4},{4,0},{1,5},{5,1},{2,6},{6,2},{3,7},{7,3},{8,12},{12,8},{9,1... | collective-permute-start | bytes 1572872 | tf_op jit(solution)/shard_map/ppermute | solution.py:21
  60.2 1.6 %collective-permute-start.14 = (bf16[1024,256]{1,0:T(8,128)(2,1)}, bf16[1024,256]{1,0:T(8,128)(2,1)}, u32[]{:S(2)}, u32[]{:S(2)}) collective-permute-start(bf16[1024,256]{1,0:T(8,128)(2,1)} %collective-permute-done.13.refs_4_), channel_id=1, source_target_pairs={{0,8},{8,0},{16,24},{24,16},{1,9},{9,1},{17,25},{25,17},{2,10},{10... | collective-permute-start | bytes 1572872 | tf_op jit(solution)/shard_map/ppermute | solution.py:21
  61.8 4.1 %shard_map.96.refs_6_ = f32[640,256]{1,0:T(8,128)} custom-call(s32[6]{0:T(128)} %stack.21.where_ref, bf16[512,7168]{1,0:T(8,128)(2,1)} %bitcast.13, bf16[512,7168]{1,0:T(8,128)(2,1)} %bitcast.14, bf16[128,7168]{1,0:T(8,128)(2,1)} %bitcast.21, bf16[128,7168]{1,0:T(8,128)(2,1)} %bitcast.22, bf16[1024,256]{1,0:T(8,128)(2,1)} %copy-done.9, ...), custom_call_target="tpu_custom_call" | custom-call | flops 671088640 | bytes 4980736 | tf_op jit(solution)/shard_map/pallas_call | solution.py:134
  66.0 1.6 %fusion.3 = (bf16[640,512]{1,0:T(8,128)(2,1)S(1)}, f32[640,512]{1,0:T(8,128)S(1)}) fusion(f32[640,512]{1,0:T(8,128)S(1)} %copy-done.1, f32[640,512]{1,0:T(8,128)} %collective-permute-done), kind=kLoop, calls=%fused_computation.11 | loop fusion | flops 655360 | bytes 4587520 | tf_op jit(solution)/shard_map/convert_element_type | solution.py:329
  67.7 1.6 %collective-permute-start.1 = (bf16[640,512]{1,0:T(8,128)(2,1)S(1)}, bf16[640,512]{1,0:T(8,128)(2,1)S(1)}, u32[]{:S(2)}, u32[]{:S(2)}) collective-permute-start(bf16[640,512]{1,0:T(8,128)(2,1)S(1)} %get-tuple-element.39), channel_id=1, source_target_pairs={{0,2},{1,3},{2,0},{3,1},{4,6},{5,7},{6,4},{7,5},{8,10},{9,11},{10,... | collective-permute-start | bytes 1966088 | tf_op jit(solution)/shard_map/ppermute | solution.py:21
  69.3 4.5 %shard_map.97.refs_6_ = f32[640,256]{1,0:T(8,128)} custom-call(s32[6]{0:T(128)} %stack.21.where_ref, bf16[512,7168]{1,0:T(8,128)(2,1)} %bitcast.15, bf16[512,7168]{1,0:T(8,128)(2,1)} %bitcast.16, bf16[128,7168]{1,0:T(8,128)(2,1)} %bitcast.23, bf16[128,7168]{1,0:T(8,128)(2,1)} %bitcast.24, bf16[1024,256]{1,0:T(8,128)(2,1)} %collective-permute-done.16.refs_4_, ...), custom_call_target="tpu_custom_call" | custom-call | flops 671088640 | bytes 4980736 | tf_op jit(solution)/shard_map/pallas_call | solution.py:134
  73.8 4.5 %shard_map.98.refs_3_ = f32[640,256]{1,0:T(8,128)} custom-call(s32[6]{0:T(128)} %stack.21.where_ref, bf16[512,7168]{1,0:T(8,128)(2,1)} %bitcast.17, bf16[512,7168]{1,0:T(8,128)(2,1)} %bitcast.18, bf16[128,7168]{1,0:T(8,128)(2,1)} %bitcast.25, bf16[128,7168]{1,0:T(8,128)(2,1)} %bitcast.26, bf16[1024,256]{1,0:T(8,128)(2,1)} %collective-permute-done.13.refs_4_, ...), custom_call_target="tpu_custom_call" | custom-call | flops 671088640 | bytes 4980736 | tf_op jit(solution)/shard_map/pallas_call | solution.py:134
  78.3 3.9 %shard_map.99 = (f32[512,256]{1,0:T(8,128)}, f32[32,256]{1,0:T(8,128)}, f32[32,256]{1,0:T(8,128)}, f32[32,256]{1,0:T(8,128)}, f32[32,256]{1,0:T(8,128)}) custom-call(s32[6]{0:T(128)} %stack.21.where_ref, bf16[512,7168]{1,0:T(8,128)(2,1)} %bitcast.19, bf16[128,7168]{1,0:T(8,128)(2,1)} %bitcast.27, bf16[1024,256]{1,0:T(8,128)(2,1)} %collective-permute-done.14.refs_2_, ...), custom_call_target="tpu_custom_call" | custom-call | flops 335544320 | bytes 3145728 | tf_op jit(solution)/shard_map/pallas_call | solution.py:134
  82.6 1.5 %collective-permute-start.23 = (f32[32,256]{1,0:T(8,128)}, f32[32,256]{1,0:T(8,128)S(1)}, u32[]{:S(2)}, u32[]{:S(2)}) collective-permute-start(f32[32,256]{1,0:T(8,128)} %get-tuple-element.33), channel_id=1, source_target_pairs={{0,2},{1,3},{2,0},{3,1},{4,6},{5,7},{6,4},{7,5},{8,10},{9,11},{10,... | collective-permute-start | bytes 98312 | tf_op jit(solution)/shard_map/ppermute | solution.py:21
  84.2 1.2 fusion.2
  86.9 1.4 %collective-permute-start.5 = (bf16[640,256]{1,0:T(8,128)(2,1)S(1)}, bf16[640,256]{1,0:T(8,128)(2,1)S(1)}, u32[]{:S(2)}, u32[]{:S(2)}) collective-permute-start(bf16[640,256]{1,0:T(8,128)(2,1)S(1)} %get-tuple-element.37), channel_id=1, source_target_pairs={{0,2},{1,3},{2,0},{3,1},{4,6},{5,7},{6,4},{7,5},{8,10},{9,11},{10,... | collective-permute-start | bytes 983048 | tf_op jit(solution)/shard_map/ppermute | solution.py:21
  88.3 2.8 %collective-permute-start.27 = (bf16[1,32,256]{2,1,0:T(8,128)(2,1)S(1)}, bf16[1,32,256]{2,1,0:T(8,128)(2,1)S(1)}, u32[]{:S(2)}, u32[]{:S(2)}) collective-permute-start(bf16[1,32,256]{2,1,0:T(8,128)(2,1)S(1)} %fusion), channel_id=1, source_target_pairs={{0,24},{8,16},{16,8},{24,0},{1,25},{9,17},{17,9},{25,1},{2,26},{10... | collective-permute-start | bytes 49160 | tf_op jit(solution)/shard_map/ppermute | solution.py:21
  91.2 4.9 %collective-permute-done.5.in_b = bf16[640,256]{1,0:T(8,128)(2,1)S(1)} collective-permute-done((bf16[640,256]{1,0:T(8,128)(2,1)S(1)}, bf16[640,256]{1,0:T(8,128)(2,1)S(1)}, u32[]{:S(2)}, u32[]{:S(2)}) %collective-permute-start.5) | collective-permute-done | bytes 327712 | tf_op jit(solution)/shard_map/ppermute | solution.py:21
  96.1 3.3 %collective-permute-start.8 = (bf16[1,32,768]{2,1,0:T(8,128)(2,1)S(1)}, bf16[1,32,768]{2,1,0:T(8,128)(2,1)S(1)}, u32[]{:S(2)}, u32[]{:S(2)}) collective-permute-start(bf16[1,32,768]{2,1,0:T(8,128)(2,1)S(1)} %maximum_bitcast_fusion), channel_id=1, source_target_pairs={{0,24},{8,16},{16,8},{24,0},{1,25},{9,17},{17,9},{25,1},{2,26},{10... | collective-permute-start | bytes 147464 | tf_op jit(solution)/shard_map/ppermute | solution.py:21
  99.4 1.1 collective-permute-start.6
  100.6 0.9 fusion.1
  101.5 1.0 collective-permute-start.11
  102.4 2.1 %collective-permute-done.7 = bf16[1,32,768]{2,1,0:T(8,128)(2,1)S(1)} collective-permute-done((bf16[1,32,768]{2,1,0:T(8,128)(2,1)S(1)}, bf16[1,32,768]{2,1,0:T(8,128)(2,1)S(1)}, u32[]{:S(2)}, u32[]{:S(2)}) %collective-permute-start.7) | collective-permute-done | bytes 49184 | tf_op jit(solution)/shard_map/ppermute | solution.py:21
  104.5 0.8 collective-permute-start.21
  105.4 2.9 %collective-permute-done.25 = bf16[1,32,256]{2,1,0:T(8,128)(2,1)S(1)} collective-permute-done((bf16[1,32,256]{2,1,0:T(8,128)(2,1)S(1)}, bf16[1,32,256]{2,1,0:T(8,128)(2,1)S(1)}, u32[]{:S(2)}, u32[]{:S(2)}) %collective-permute-start.25) | collective-permute-done | bytes 16416 | tf_op jit(solution)/shard_map/ppermute | solution.py:21
  108.2 1.2 collective-permute-start.9
  109.5 0.9 collective-permute-start.28
  110.4 3.9 %collective-permute-done.12.refs_3_ = f32[128,512]{1,0:T(8,128)S(1)} collective-permute-done((f32[128,512]{1,0:T(8,128)S(1)}, f32[128,512]{1,0:T(8,128)S(1)}, u32[]{:S(2)}, u32[]{:S(2)}) %collective-permute-start.12) | collective-permute-done | bytes 262176 | tf_op jit(solution)/shard_map/ppermute | solution.py:21
  114.3 0.7 copy-done.16
  115.6 3.9 %shard_map.93 = (f32[128,256]{1,0:T(8,128)}, f32[4,256]{1,0:T(4,128)}, bf16[2,512,256]{2,1,0:T(8,128)(2,1)}, bf16[2,256,256]{2,1,0:T(8,128)(2,1)}, f32[2,256,256]{2,1,0:T(8,128)}) custom-call(s32[6]{0:T(128)} %stack.21.where_ref, f32[640,512]{1,0:T(8,128)} %copy-done, bf16[640,512]{1,0:T(8,128)(2,1)} %copy-done.7, f32[640,256]{1,0:T(8,128)} %copy-done.2, ...), custom_call_target="tpu_custom_call" | custom-call | tf_op jit(solution)/shard_map/pallas_call | solution.py:214
  119.6 0.7 copy-done.17
  120.3 2.9 %shard_map.100 = (f32[128,256]{1,0:T(8,128)}, f32[4,256]{1,0:T(4,128)}) custom-call(s32[6]{0:T(128)} %stack.21.where_ref, f32[512,256]{1,0:T(8,128)} %get-tuple-element.36.out_a, bf16[512,256]{1,0:T(8,128)(2,1)} %copy-done.17, bf16[2,512,256]{2,1,0:T(8,128)(2,1)} %get-tuple-element.26.ins_ref, bf16[2,256,256]{2,1,0:T(8,128)(2,1)} %get-tuple-element.27.qins_ref, ...), custom_call_target="tpu_custom_call" | custom-call | tf_op jit(solution)/shard_map/pallas_call | solution.py:243
  123.8 1.7 %shard_map.101 = f32[8,128]{1,0:T(8,128)} custom-call(s32[6]{0:T(128)} %stack.21.where_ref, f32[128,256]{1,0:T(8,128)} %get-tuple-element.20.far_ref, f32[4,256]{1,0:T(4,128)} %get-tuple-element.21.part_a, f32[128,256]{1,0:T(8,128)} %get-tuple-element.29.near_ref, f32[4,256]{1,0:T(4,128)} %get-tuple-element.30.part_b, bf16[4,32,256]{2,1,0:T(8,128)(2,1)} %copy-done.18, ...), custom_call_target="tpu_custom_call" | custom-call | tf_op jit(solution)/shard_map/pallas_call | solution.py:276
  125.5 1.2 collective-permute-start.30
  126.7 1.6 %collective-permute-start.31 = (f32[8,128]{1,0:T(8,128)}, f32[8,128]{1,0:T(8,128)S(1)}, u32[]{:S(2)}, u32[]{:S(2)}) collective-permute-start(f32[8,128]{1,0:T(8,128)} %shard_map.101), channel_id=1, source_target_pairs={{0,3},{1,2},{2,1},{3,0},{4,7},{5,6},{6,5},{7,4},{8,11},{9,10},{10,... | collective-permute-start | bytes 12296 | tf_op jit(solution)/shard_map/ppermute | solution.py:21
  128.3 1.0 collective-permute-done.30
  129.9 0.7 add_add_fusion
  (82 shorter events, 4.9 us)
Async XLA Ops:
  0.0 9.5 %copy-start.4 = (bf16[2048,256]{1,0:T(8,128)(2,1)S(1)}, bf16[2048,256]{1,0:T(8,128)(2,1)}, u32[]{:S(2)}) copy-start(bf16[2048,256]{1,0:T(8,128)(2,1)} %bi.1) | copy-start | bytes 3145732
  9.2 56.7 %collective-permute-start = (f32[640,512]{1,0:T(8,128)}, f32[640,512]{1,0:T(8,128)}, u32[]{:S(2)}, u32[]{:S(2)}) collective-permute-start(f32[640,512]{1,0:T(8,128)} %shard_map.91), channel_id=1, source_target_pairs={{0,1},{1,0},{2,3},{3,2},{4,5},{5,4},{6,7},{7,6},{8,9},{9,8},{10,11... | collective-permute-start | bytes 3932168 | tf_op jit(solution)/shard_map/ppermute | solution.py:21
  9.5 15.3 %collective-permute-start.2 = (bf16[1024,256]{1,0:T(8,128)(2,1)S(1)}, bf16[1024,256]{1,0:T(8,128)(2,1)S(1)}, u32[]{:S(2)}, u32[]{:S(2)}) collective-permute-start(bf16[1024,256]{1,0:T(8,128)(2,1)S(1)} %constant_dynamic-slice_fusion), channel_id=1, source_target_pairs={{0,4},{4,0},{1,5},{5,1},{2,6},{6,2},{3,7},{7,3},{8,12},{12,8},{9,1... | collective-permute-start | bytes 1572872 | tf_op jit(solution)/shard_map/ppermute | solution.py:21
  16.5 19.6 %collective-permute-start.18 = (bf16[1024,256]{1,0:T(8,128)(2,1)}, bf16[1024,256]{1,0:T(8,128)(2,1)S(1)}, u32[]{:S(2)}, u32[]{:S(2)}) collective-permute-start(bf16[1024,256]{1,0:T(8,128)(2,1)} %shard_map.95), channel_id=1, source_target_pairs={{0,4},{4,0},{1,5},{5,1},{2,6},{6,2},{3,7},{7,3},{8,12},{12,8},{9,1... | collective-permute-start | bytes 1572872 | tf_op jit(solution)/shard_map/ppermute | solution.py:21
  19.5 27.9 %collective-permute-start.16 = (bf16[1024,256]{1,0:T(8,128)(2,1)}, bf16[1024,256]{1,0:T(8,128)(2,1)}, u32[]{:S(2)}, u32[]{:S(2)}) collective-permute-start(bf16[1024,256]{1,0:T(8,128)(2,1)} %get-tuple-element.24), channel_id=1, source_target_pairs={{0,4},{4,0},{1,5},{5,1},{2,6},{6,2},{3,7},{7,3},{8,12},{12,8},{9,1... | collective-permute-start | bytes 1572872 | tf_op jit(solution)/shard_map/ppermute | solution.py:21
  24.8 24.7 %copy-start.11 = (bf16[1024,256]{1,0:T(8,128)(2,1)}, bf16[1024,256]{1,0:T(8,128)(2,1)S(1)}, u32[]{:S(2)}) copy-start(bf16[1024,256]{1,0:T(8,128)(2,1)S(1)} %collective-permute-done.2.refs_4_) | copy-start | bytes 1572868
  24.8 24.7 %collective-permute-start.3 = (bf16[1024,256]{1,0:T(8,128)(2,1)S(1)}, bf16[1024,256]{1,0:T(8,128)(2,1)S(1)}, u32[]{:S(2)}, u32[]{:S(2)}) collective-permute-start(bf16[1024,256]{1,0:T(8,128)(2,1)S(1)} %collective-permute-done.2.refs_4_), channel_id=1, source_target_pairs={{0,8},{8,0},{16,24},{24,16},{1,9},{9,1},{17,25},{25,17},{2,10},{10... | collective-permute-start | bytes 1572872 | tf_op jit(solution)/shard_map/ppermute | solution.py:21
  26.9 31.5 %collective-permute-start.13 = (bf16[1024,256]{1,0:T(8,128)(2,1)}, bf16[1024,256]{1,0:T(8,128)(2,1)}, u32[]{:S(2)}, u32[]{:S(2)}) collective-permute-start(bf16[1024,256]{1,0:T(8,128)(2,1)} %get-tuple-element.22), channel_id=1, source_target_pairs={{0,4},{4,0},{1,5},{5,1},{2,6},{6,2},{3,7},{7,3},{8,12},{12,8},{9,1... | collective-permute-start | bytes 1572872 | tf_op jit(solution)/shard_map/ppermute | solution.py:21
  36.1 18.4 %copy-start.9 = (bf16[1024,256]{1,0:T(8,128)(2,1)}, bf16[1024,256]{1,0:T(8,128)(2,1)S(1)}, u32[]{:S(2)}) copy-start(bf16[1024,256]{1,0:T(8,128)(2,1)S(1)} %collective-permute-done.18.refs_4_) | copy-start | bytes 1572868
  36.1 24.1 %collective-permute-start.19 = (bf16[1024,256]{1,0:T(8,128)(2,1)S(1)}, bf16[1024,256]{1,0:T(8,128)(2,1)S(1)}, u32[]{:S(2)}, u32[]{:S(2)}) collective-permute-start(bf16[1024,256]{1,0:T(8,128)(2,1)S(1)} %collective-permute-done.18.refs_4_), channel_id=1, source_target_pairs={{0,8},{8,0},{16,24},{24,16},{1,9},{9,1},{17,25},{25,17},{2,10},{10... | collective-permute-start | bytes 1572872 | tf_op jit(solution)/shard_map/ppermute | solution.py:21
  47.4 20.3 %collective-permute-start.17 = (bf16[1024,256]{1,0:T(8,128)(2,1)}, bf16[1024,256]{1,0:T(8,128)(2,1)}, u32[]{:S(2)}, u32[]{:S(2)}) collective-permute-start(bf16[1024,256]{1,0:T(8,128)(2,1)} %collective-permute-done.16.refs_4_), channel_id=1, source_target_pairs={{0,8},{8,0},{16,24},{24,16},{1,9},{9,1},{17,25},{25,17},{2,10},{10... | collective-permute-start | bytes 1572872 | tf_op jit(solution)/shard_map/ppermute | solution.py:21
  54.4 29.7 %collective-permute-start.4 = (f32[640,256]{1,0:T(8,128)}, f32[640,256]{1,0:T(8,128)}, u32[]{:S(2)}, u32[]{:S(2)}) collective-permute-start(f32[640,256]{1,0:T(8,128)} %shard_map.92), channel_id=1, source_target_pairs={{0,1},{1,0},{2,3},{3,2},{4,5},{5,4},{6,7},{7,6},{8,9},{9,8},{10,11... | collective-permute-start | bytes 1966088 | tf_op jit(solution)/shard_map/ppermute | solution.py:21
  58.4 15.4 %collective-permute-start.15 = (bf16[1024,256]{1,0:T(8,128)(2,1)}, bf16[1024,256]{1,0:T(8,128)(2,1)}, u32[]{:S(2)}, u32[]{:S(2)}) collective-permute-start(bf16[1024,256]{1,0:T(8,128)(2,1)} %get-tuple-element.23), channel_id=1, source_target_pairs={{0,4},{4,0},{1,5},{5,1},{2,6},{6,2},{3,7},{7,3},{8,12},{12,8},{9,1... | collective-permute-start | bytes 1572872 | tf_op jit(solution)/shard_map/ppermute | solution.py:21
  60.2 5.8 %copy-start.14 = (f32[128,512]{1,0:T(8,128)S(1)}, f32[128,512]{1,0:T(8,128)}, u32[]{:S(2)}) copy-start(f32[128,512]{1,0:T(8,128)} %refs_0_.3) | copy-start | bytes 786436
  60.2 5.8 %copy-start.1 = (f32[640,512]{1,0:T(8,128)S(1)}, f32[640,512]{1,0:T(8,128)}, u32[]{:S(2)}) copy-start(f32[640,512]{1,0:T(8,128)} %shard_map.91) | copy-start | bytes 3932164
  60.2 1.7 %copy-start.10 = (bf16[1024,256]{1,0:T(8,128)(2,1)}, bf16[1024,256]{1,0:T(8,128)(2,1)S(1)}, u32[]{:S(2)}) copy-start(bf16[1024,256]{1,0:T(8,128)(2,1)S(1)} %collective-permute-done.19.refs_5_) | copy-start | bytes 1572868
  60.2 18.1 %collective-permute-start.14 = (bf16[1024,256]{1,0:T(8,128)(2,1)}, bf16[1024,256]{1,0:T(8,128)(2,1)}, u32[]{:S(2)}, u32[]{:S(2)}) collective-permute-start(bf16[1024,256]{1,0:T(8,128)(2,1)} %collective-permute-done.13.refs_4_), channel_id=1, source_target_pairs={{0,8},{8,0},{16,24},{24,16},{1,9},{9,1},{17,25},{25,17},{2,10},{10... | collective-permute-start | bytes 1572872 | tf_op jit(solution)/shard_map/ppermute | solution.py:21
  65.9 43.6 %collective-permute-start.10 = (f32[128,512]{1,0:T(8,128)S(1)}, f32[128,512]{1,0:T(8,128)}, u32[]{:S(2)}, u32[]{:S(2)}) collective-permute-start(f32[128,512]{1,0:T(8,128)S(1)} %copy-done.14), channel_id=1, source_target_pairs={{0,1},{1,0},{2,3},{3,2},{4,5},{5,4},{6,7},{7,6},{8,9},{9,8},{10,11... | collective-permute-start | bytes 786440 | tf_op jit(solution)/shard_map/ppermute | solution.py:21
  67.7 23.5 %copy-start = (f32[640,512]{1,0:T(8,128)}, f32[640,512]{1,0:T(8,128)S(1)}, u32[]{:S(2)}) copy-start(f32[640,512]{1,0:T(8,128)S(1)} %get-tuple-element.40.own_a) | copy-start | bytes 3932164
  67.7 23.5 %collective-permute-start.1 = (bf16[640,512]{1,0:T(8,128)(2,1)S(1)}, bf16[640,512]{1,0:T(8,128)(2,1)S(1)}, u32[]{:S(2)}, u32[]{:S(2)}) collective-permute-start(bf16[640,512]{1,0:T(8,128)(2,1)S(1)} %get-tuple-element.39), channel_id=1, source_target_pairs={{0,2},{1,3},{2,0},{3,1},{4,6},{5,7},{6,4},{7,5},{8,10},{9,11},{10,... | collective-permute-start | bytes 1966088 | tf_op jit(solution)/shard_map/ppermute | solution.py:21
  78.3 5.9 %copy-start.3 = (f32[640,256]{1,0:T(8,128)S(1)}, f32[640,256]{1,0:T(8,128)}, u32[]{:S(2)}) copy-start(f32[640,256]{1,0:T(8,128)} %shard_map.92) | copy-start | bytes 1966084
  82.3 3.6 %copy-start.8 = (f32[512,256]{1,0:T(8,128)S(1)}, f32[512,256]{1,0:T(8,128)}, u32[]{:S(2)}) copy-start(f32[512,256]{1,0:T(8,128)} %get-tuple-element.25) | copy-start | bytes 1572868
  82.3 6.0 %copy-start.20 = (f32[32,256]{1,0:T(8,128)S(1)}, f32[32,256]{1,0:T(8,128)}, u32[]{:S(2)}) copy-start(f32[32,256]{1,0:T(8,128)} %get-tuple-element.31) | copy-start | bytes 98308
  82.3 3.6 %collective-permute-start.24 = (f32[32,256]{1,0:T(8,128)}, f32[32,256]{1,0:T(8,128)S(1)}, u32[]{:S(2)}, u32[]{:S(2)}) collective-permute-start(f32[32,256]{1,0:T(8,128)} %get-tuple-element.34), channel_id=1, source_target_pairs={{0,3},{1,2},{2,1},{3,0},{4,7},{5,6},{6,5},{7,4},{8,11},{9,10},{10,... | collective-permute-start | bytes 98312 | tf_op jit(solution)/shard_map/ppermute | solution.py:21
  82.6 4.3 %collective-permute-start.23 = (f32[32,256]{1,0:T(8,128)}, f32[32,256]{1,0:T(8,128)S(1)}, u32[]{:S(2)}, u32[]{:S(2)}) collective-permute-start(f32[32,256]{1,0:T(8,128)} %get-tuple-element.33), channel_id=1, source_target_pairs={{0,2},{1,3},{2,0},{3,1},{4,6},{5,7},{6,4},{7,5},{8,10},{9,11},{10,... | collective-permute-start | bytes 98312 | tf_op jit(solution)/shard_map/ppermute | solution.py:21
  84.2 4.1 %collective-permute-start.22 = (f32[32,256]{1,0:T(8,128)}, f32[32,256]{1,0:T(8,128)S(1)}, u32[]{:S(2)}, u32[]{:S(2)}) collective-permute-start(f32[32,256]{1,0:T(8,128)} %get-tuple-element.32), channel_id=1, source_target_pairs={{0,1},{1,0},{2,3},{3,2},{4,5},{5,4},{6,7},{7,6},{8,9},{9,8},{10,11... | collective-permute-start | bytes 98312 | tf_op jit(solution)/shard_map/ppermute | solution.py:21
  85.4 20.0 %copy-start.2 = (f32[640,256]{1,0:T(8,128)}, f32[640,256]{1,0:T(8,128)S(1)}, u32[]{:S(2)}) copy-start(f32[640,256]{1,0:T(8,128)S(1)} %get-tuple-element.38.in_a) | copy-start | bytes 1966084
  85.9 13.5 %collective-permute-start.20 = (f32[512,256]{1,0:T(8,128)S(1)}, f32[512,256]{1,0:T(8,128)S(1)}, u32[]{:S(2)}, u32[]{:S(2)}) collective-permute-start(f32[512,256]{1,0:T(8,128)S(1)} %copy-done.8), channel_id=1, source_target_pairs={{0,1},{1,0},{2,3},{3,2},{4,5},{5,4},{6,7},{7,6},{8,9},{9,8},{10,11... | collective-permute-start | bytes 1572872 | tf_op jit(solution)/shard_map/ppermute | solution.py:21
  86.9 9.2 %collective-permute-start.5 = (bf16[640,256]{1,0:T(8,128)(2,1)S(1)}, bf16[640,256]{1,0:T(8,128)(2,1)S(1)}, u32[]{:S(2)}, u32[]{:S(2)}) collective-permute-start(bf16[640,256]{1,0:T(8,128)(2,1)S(1)} %get-tuple-element.37), channel_id=1, source_target_pairs={{0,2},{1,3},{2,0},{3,1},{4,6},{5,7},{6,4},{7,5},{8,10},{9,11},{10,... | collective-permute-start | bytes 983048 | tf_op jit(solution)/shard_map/ppermute | solution.py:21
  88.3 11.1 %collective-permute-start.27 = (bf16[1,32,256]{2,1,0:T(8,128)(2,1)S(1)}, bf16[1,32,256]{2,1,0:T(8,128)(2,1)S(1)}, u32[]{:S(2)}, u32[]{:S(2)}) collective-permute-start(bf16[1,32,256]{2,1,0:T(8,128)(2,1)S(1)} %fusion), channel_id=1, source_target_pairs={{0,24},{8,16},{16,8},{24,0},{1,25},{9,17},{17,9},{25,1},{2,26},{10... | collective-permute-start | bytes 49160 | tf_op jit(solution)/shard_map/ppermute | solution.py:21
  91.2 18.3 %copy-start.7 = (bf16[640,512]{1,0:T(8,128)(2,1)}, bf16[640,512]{1,0:T(8,128)(2,1)S(1)}, u32[]{:S(2)}) copy-start(bf16[640,512]{1,0:T(8,128)(2,1)S(1)} %collective-permute-done.1.own_b) | copy-start | bytes 1966084
  91.2 10.3 %collective-permute-start.26 = (bf16[1,32,256]{2,1,0:T(8,128)(2,1)S(1)}, bf16[1,32,256]{2,1,0:T(8,128)(2,1)S(1)}, u32[]{:S(2)}, u32[]{:S(2)}) collective-permute-start(bf16[1,32,256]{2,1,0:T(8,128)(2,1)S(1)} %fusion), channel_id=1, source_target_pairs={{0,16},{8,24},{16,0},{24,8},{1,17},{9,25},{17,1},{25,9},{2,18},{10... | collective-permute-start | bytes 49160 | tf_op jit(solution)/shard_map/ppermute | solution.py:21
  96.1 3.3 %copy-start.13 = (bf16[640,256]{1,0:T(8,128)(2,1)}, bf16[640,256]{1,0:T(8,128)(2,1)S(1)}, u32[]{:S(2)}) copy-start(bf16[640,256]{1,0:T(8,128)(2,1)S(1)} %collective-permute-done.5.in_b) | copy-start | bytes 983044
  96.1 6.3 %collective-permute-start.8 = (bf16[1,32,768]{2,1,0:T(8,128)(2,1)S(1)}, bf16[1,32,768]{2,1,0:T(8,128)(2,1)S(1)}, u32[]{:S(2)}, u32[]{:S(2)}) collective-permute-start(bf16[1,32,768]{2,1,0:T(8,128)(2,1)S(1)} %maximum_bitcast_fusion), channel_id=1, source_target_pairs={{0,24},{8,16},{16,8},{24,0},{1,25},{9,17},{17,9},{25,1},{2,26},{10... | collective-permute-start | bytes 147464 | tf_op jit(solution)/shard_map/ppermute | solution.py:21
  99.4 5.1 %collective-permute-start.7 = (bf16[1,32,768]{2,1,0:T(8,128)(2,1)S(1)}, bf16[1,32,768]{2,1,0:T(8,128)(2,1)S(1)}, u32[]{:S(2)}, u32[]{:S(2)}) collective-permute-start(bf16[1,32,768]{2,1,0:T(8,128)(2,1)S(1)} %maximum_bitcast_fusion), channel_id=1, source_target_pairs={{0,16},{8,24},{16,0},{24,8},{1,17},{9,25},{17,1},{25,9},{2,18},{10... | collective-permute-start | bytes 147464 | tf_op jit(solution)/shard_map/ppermute | solution.py:21
  99.4 5.1 %collective-permute-start.6 = (bf16[1,32,768]{2,1,0:T(8,128)(2,1)S(1)}, bf16[1,32,768]{2,1,0:T(8,128)(2,1)S(1)}, u32[]{:S(2)}, u32[]{:S(2)}) collective-permute-start(bf16[1,32,768]{2,1,0:T(8,128)(2,1)S(1)} %maximum_bitcast_fusion), channel_id=1, source_target_pairs={{0,8},{8,0},{16,24},{24,16},{1,9},{9,1},{17,25},{25,17},{2,10},{10... | collective-permute-start | bytes 147464 | tf_op jit(solution)/shard_map/ppermute | solution.py:21
  101.5 8.9 %collective-permute-start.11 = (f32[128,512]{1,0:T(8,128)S(1)}, f32[128,512]{1,0:T(8,128)S(1)}, u32[]{:S(2)}, u32[]{:S(2)}) collective-permute-start(f32[128,512]{1,0:T(8,128)S(1)} %copy-done.14), channel_id=1, source_target_pairs={{0,2},{1,3},{2,0},{3,1},{4,6},{5,7},{6,4},{7,5},{8,10},{9,11},{10,... | collective-permute-start | bytes 786440 | tf_op jit(solution)/shard_map/ppermute | solution.py:21
  102.4 11.8 %collective-permute-start.12 = (f32[128,512]{1,0:T(8,128)S(1)}, f32[128,512]{1,0:T(8,128)S(1)}, u32[]{:S(2)}, u32[]{:S(2)}) collective-permute-start(f32[128,512]{1,0:T(8,128)S(1)} %copy-done.14), channel_id=1, source_target_pairs={{0,3},{1,2},{2,1},{3,0},{4,7},{5,6},{6,5},{7,4},{8,11},{9,10},{10,... | collective-permute-start | bytes 786440 | tf_op jit(solution)/shard_map/ppermute | solution.py:21
  104.5 3.7 %collective-permute-start.25 = (bf16[1,32,256]{2,1,0:T(8,128)(2,1)S(1)}, bf16[1,32,256]{2,1,0:T(8,128)(2,1)S(1)}, u32[]{:S(2)}, u32[]{:S(2)}) collective-permute-start(bf16[1,32,256]{2,1,0:T(8,128)(2,1)S(1)} %fusion), channel_id=1, source_target_pairs={{0,8},{8,0},{16,24},{24,16},{1,9},{9,1},{17,25},{25,17},{2,10},{10... | collective-permute-start | bytes 49160 | tf_op jit(solution)/shard_map/ppermute | solution.py:21
  104.5 15.0 %collective-permute-start.21 = (bf16[512,256]{1,0:T(8,128)(2,1)S(1)}, bf16[512,256]{1,0:T(8,128)(2,1)S(1)}, u32[]{:S(2)}, u32[]{:S(2)}) collective-permute-start(bf16[512,256]{1,0:T(8,128)(2,1)S(1)} %get-tuple-element.35), channel_id=1, source_target_pairs={{0,2},{1,3},{2,0},{3,1},{4,6},{5,7},{6,4},{7,5},{8,10},{9,11},{10,... | collective-permute-start | bytes 786440 | tf_op jit(solution)/shard_map/ppermute | solution.py:21
  105.4 8.9 %copy-start.6 = (bf16[4,32,768]{2,1,0:T(8,128)(2,1)}, bf16[4,32,768]{2,1,0:T(8,128)(2,1)S(1)}, u32[]{:S(2)}) copy-start(bf16[4,32,768]{2,1,0:T(8,128)(2,1)S(1)} %pad_maximum_fusion.qa) | copy-start | bytes 589828
  108.2 6.0 %collective-permute-start.9 = (bf16[4,32,768]{2,1,0:T(8,128)(2,1)S(1)}, bf16[4,32,768]{2,1,0:T(8,128)(2,1)S(1)}, u32[]{:S(2)}, u32[]{:S(2)}) collective-permute-start(bf16[4,32,768]{2,1,0:T(8,128)(2,1)S(1)} %pad_maximum_fusion.qa), channel_id=1, source_target_pairs={{0,4},{4,0},{1,5},{5,1},{2,6},{6,2},{3,7},{7,3},{8,12},{12,8},{9,1... | collective-permute-start | bytes 589832 | tf_op jit(solution)/shard_map/ppermute | solution.py:21
  109.5 13.7 %copy-start.18 = (bf16[4,32,256]{2,1,0:T(8,128)(2,1)}, bf16[4,32,256]{2,1,0:T(8,128)(2,1)S(1)}, u32[]{:S(2)}) copy-start(bf16[4,32,256]{2,1,0:T(8,128)(2,1)S(1)} %pad_maximum_fusion.1.la) | copy-start | bytes 196612
  109.5 13.7 %collective-permute-start.28 = (bf16[4,32,256]{2,1,0:T(8,128)(2,1)S(1)}, bf16[4,32,256]{2,1,0:T(8,128)(2,1)S(1)}, u32[]{:S(2)}, u32[]{:S(2)}) collective-permute-start(bf16[4,32,256]{2,1,0:T(8,128)(2,1)S(1)} %pad_maximum_fusion.1.la), channel_id=1, source_target_pairs={{0,4},{4,0},{1,5},{5,1},{2,6},{6,2},{3,7},{7,3},{8,12},{12,8},{9,1... | collective-permute-start | bytes 196616 | tf_op jit(solution)/shard_map/ppermute | solution.py:21
  110.4 3.9 %copy-start.15 = (f32[128,512]{1,0:T(8,128)}, f32[128,512]{1,0:T(8,128)S(1)}, u32[]{:S(2)}) copy-start(f32[128,512]{1,0:T(8,128)S(1)} %collective-permute-done.11.refs_2_) | copy-start | bytes 786436
  125.5 3.8 %collective-permute-start.30 = (f32[8,128]{1,0:T(8,128)}, f32[8,128]{1,0:T(8,128)S(1)}, u32[]{:S(2)}, u32[]{:S(2)}) collective-permute-start(f32[8,128]{1,0:T(8,128)} %shard_map.101), channel_id=1, source_target_pairs={{0,2},{1,3},{2,0},{3,1},{4,6},{5,7},{6,4},{7,5},{8,10},{9,11},{10,... | collective-permute-start | bytes 12296 | tf_op jit(solution)/shard_map/ppermute | solution.py:21
  126.7 3.2 %collective-permute-start.31 = (f32[8,128]{1,0:T(8,128)}, f32[8,128]{1,0:T(8,128)S(1)}, u32[]{:S(2)}, u32[]{:S(2)}) collective-permute-start(f32[8,128]{1,0:T(8,128)} %shard_map.101), channel_id=1, source_target_pairs={{0,3},{1,2},{2,1},{3,0},{4,7},{5,6},{6,5},{7,4},{8,11},{9,10},{10,... | collective-permute-start | bytes 12296 | tf_op jit(solution)/shard_map/ppermute | solution.py:21
  128.3 1.6 %collective-permute-start.29 = (f32[8,128]{1,0:T(8,128)}, f32[8,128]{1,0:T(8,128)S(1)}, u32[]{:S(2)}, u32[]{:S(2)}) collective-permute-start(f32[8,128]{1,0:T(8,128)} %shard_map.101), channel_id=1, source_target_pairs={{0,1},{1,0},{2,3},{3,2},{4,5},{5,4},{6,7},{7,6},{8,9},{9,8},{10,11... | collective-permute-start | bytes 12296 | tf_op jit(solution)/shard_map/ppermute | solution.py:21
  (5 other events, 3.5 us)
